TPU v7x, 256 devices: a whole 4x4x8 slice. The times are simulated.
256 devices in a mesh: row: 32 (over x, y, core), col: 8 (over z).
Axes of the slice: x: 4, y: 4, z: 8, core: 2. Of those that a mesh axis runs over, the one named last changes fastest.
Arguments:
- matrix: float32 [65536, 5, 8, 128], P('row', None, 'col'), may hold values from -320 to 320, as said below
Outputs:
- r_rows: float32 [256, 5, 8, 128], P(None, None, 'col')
- residual: float32 [65536, 5, 8, 128], P('row', None, 'col')
Inputs may be any that keep to these rules, and one draw needn't show every extreme that they name: `matrix`: real entries; the first 256 columns have full column rank on every block of 2048 rows.
All inputs are finite; a program needn't handle non-finite values.
Results may differ from a plain program's by a relative error of at most 0.0003.
Values sent between devices are 32-bit elements; how exact they have to be, the bound alone decides.
No kernel may reach another device: no remote copies, remote signals or barrier semaphores. Data moves between devices by JAX's collectives and lax.ppermute only.
A program may use at most 128 MiB of HBM per device.

v0:
```python
import functools
import math

import jax
import jax.numpy as jnp
from jax import lax
from jax.experimental import pallas as pl
from jax.experimental.pallas import tpu as pltpu
from jax.sharding import PartitionSpec as P

LANES = 128
STEP = 32
GROUP = 4
SPAN = 64
HIGHEST = lax.Precision.HIGHEST


def split(value):
    high = value.astype(jnp.bfloat16)
    low = (value - high.astype(jnp.float32)).astype(jnp.bfloat16)
    return high, low


def contract(left, right, dims, precision=None):
    return lax.dot_general(
        left, right, (dims, ((), ())), precision=precision, preferred_element_type=jnp.float32
    )


def dot3(left, right, dims):
    (lh, ll), (rh, rl) = left, right
    return contract(lh, rh, dims) + (contract(lh, rl, dims) + contract(ll, rh, dims))


def dot4(left, right, dims):
    return dot3(left, right, dims) + contract(left[1], right[1], dims)


def sources(col, hop, n_col):
    if hop == 0 or 2 * hop == n_col:
        return [lax.rem(col + hop, n_col)]
    return [lax.rem(col + n_col - hop, n_col), lax.rem(col + hop, n_col)]


def load_piece(refs):
    if len(refs) == 1:
        half = refs[0].shape[0] // 2
        return jnp.concatenate([refs[0][:half], refs[0][half:]], axis=1)
    return jnp.concatenate([refs[0][...], refs[1][...]], axis=1)


def fetch(matrix_ref, window_ref, sem, chunk, long):
    start = pl.multiple_of(chunk * long, long)
    return pltpu.make_async_copy(matrix_ref.at[pl.ds(start, long)], window_ref, sem)


def load_blocks(window_ref, rows, blocks):
    return jnp.concatenate(
        [window_ref[pl.ds(block, rows, stride=blocks), :] for block in range(blocks)], axis=1
    )


FIRST = ((0,), (0,))


def gram_kernel(piece_ref, gram_ref):
    half = piece_ref.shape[0] // 2
    left, right = split(piece_ref[:half]), split(piece_ref[half:])
    gram_ref[0] = dot4(left, left, FIRST)
    gram_ref[1] = dot4(right, right, FIRST)
    gram_ref[2] = dot4(left, right, FIRST)


def stage_kernel(blocks, matrix_ref, high_ref, low_ref, window, sems):
    chunks, long = window.shape[0], window.shape[1]
    rows = long // blocks
    copies = [fetch(matrix_ref, window.at[i], sems.at[i], i, long) for i in range(chunks)]
    for copy in copies:
        copy.start()
    for i, copy in enumerate(copies):
        copy.wait()
        for b in range(blocks):
            high, low = split(window[i, pl.ds(b, rows, stride=blocks), :])
            high_ref[i, :, LANES * b : LANES * (b + 1)] = high
            low_ref[i, :, LANES * b : LANES * (b + 1)] = low


def collect_kernel(hop, n_col, shapes, where_ref, *refs):
    pieces = []
    for count in shapes:
        pieces.append(refs[:count])
        refs = refs[count:]
    high_ref, low_ref, cross_ref = refs[0], refs[1], refs[-1]
    total = None
    for i, chunk in enumerate(sources(where_ref[0], hop, n_col)):
        panel = split(load_piece(pieces[i]))
        term = dot3(panel, (high_ref[chunk], low_ref[chunk]), FIRST)
        total = term if total is None else total + term
    for b in range(cross_ref.shape[0]):
        term = total[:, LANES * b : LANES * (b + 1)]
        cross_ref[b] = refs[2][b] + term if hop else term


def factor_kernel(begin, end, where_ref, *refs):
    if begin == 0:
        mine_ref, other_ref, work, parts = refs
        core = where_ref[1]
        count = mine_ref.shape[0]
        parts[pl.ds(pl.multiple_of(core * count, count), count)] = mine_ref[...]
        parts[pl.ds(pl.multiple_of((1 - core) * count, count), count)] = other_ref[...]
        work[:LANES, :LANES] = parts[:LANES]
        work[:LANES, LANES:] = parts[2 * LANES :]
        work[LANES:, :LANES] = jnp.zeros((LANES, LANES), jnp.float32)
        work[LANES:, LANES:] = parts[LANES : 2 * LANES]
    else:
        work_in, work = refs
        work[...] = work_in[...]
    size = work.shape[0]
    halves = size // LANES
    lane = lax.broadcasted_iota(jnp.int32, (8, LANES), 1)
    sub = lax.broadcasted_iota(jnp.int32, (8, LANES), 0)
    wide = (8, LANES)
    for begin in range(begin, end, STEP):
        tiles = [
            [work[begin + 8 * t : begin + 8 * t + 8, LANES * h : LANES * (h + 1)] for h in range(halves)]
            for t in range(STEP // 8)
        ]
        hot = begin // LANES
        for j in range(0, STEP, GROUP):
            t0, r0 = j // 8, j % 8
            l0 = (begin + j) % LANES
            below = range(t0, STEP // 8)
            cols = [
                {t: jnp.broadcast_to(tiles[t][hot][:, l0 + q : l0 + q + 1], wide) for t in below}
                for q in range(GROUP)
            ]
            rows = [
                [jnp.broadcast_to(tiles[t0][h][r0 + q : r0 + q + 1], wide) for h in range(halves)]
                for q in range(GROUP)
            ]
            small = {
                (i, q): jnp.broadcast_to(cols[q][t0][r0 + i : r0 + i + 1], wide)
                for q in range(GROUP)
                for i in range(q, GROUP)
            }
            for q in range(GROUP):
                inv = lax.rsqrt(small[q, q])
                at = lane == l0 + q
                rows[q] = [v * inv for v in rows[q]]
                rows[q][hot] = jnp.where(at, inv, rows[q][hot])
                cols[q] = {t: v * inv for t, v in cols[q].items()}
                ell = {i: small[i, q] * inv for i in range(q + 1, GROUP)}
                for i in range(q + 1, GROUP):
                    for p in range(q + 1, i + 1):
                        small[i, p] = small[i, p] - ell[i] * ell[p]
                    rows[i][hot] = jnp.where(at, 0.0, rows[i][hot])
                    rows[i] = [v - ell[i] * u for v, u in zip(rows[i], rows[q])]
                    cols[i] = {t: v - cols[q][t] * ell[i] for t, v in cols[i].items()}
            cleared = jnp.logical_and(lane >= l0, lane < l0 + GROUP)
            for q in range(GROUP - 1):
                stale = jnp.logical_and(lane > l0 + q, lane < l0 + GROUP)
                rows[q][hot] = jnp.where(stale, 0.0, rows[q][hot])
            for t in below:
                fresh = []
                for h in range(halves):
                    value = tiles[t][h]
                    if h == hot:
                        value = jnp.where(cleared, 0.0, value)
                    for q in range(GROUP):
                        value = value - cols[q][t] * rows[q][h]
                    if t == t0:
                        value = jnp.where(sub < r0, tiles[t][h], value)
                        for q in range(GROUP):
                            value = jnp.where(sub == r0 + q, rows[q][h], value)
                    fresh.append(value)
                tiles[t] = fresh
        panel = jnp.concatenate([jnp.concatenate(t, axis=1) for t in tiles], axis=0)
        column = lax.broadcasted_iota(jnp.int32, (STEP, size), 1)
        line = lax.broadcasted_iota(jnp.int32, (STEP, size), 0) + begin
        upper = jnp.logical_and(column > line, column < begin + STEP)
        panel = jnp.where(upper, 0.0, panel)
        if begin + STEP < size:
            base = (begin + STEP) // LANES * LANES
            ahead = jnp.where(column >= begin + STEP, panel, 0.0)[:, base:]
            update = contract(ahead, panel, ((0,), (0,)), HIGHEST)
            here = lax.broadcasted_iota(jnp.int32, (size - base, size), 1)
            old = jnp.where(jnp.logical_and(here >= begin, here < begin + STEP), 0.0, work[base:, :])
            work[base:, :] = old - update
        work[begin : begin + STEP, :] = jnp.where(column < begin + STEP, panel, 0.0)


def residual_kernel(n_col, blocks, scale, shapes, where_ref, *refs):
    pieces = []
    for count in shapes:
        pieces.append(refs[:count])
        refs = refs[count:]
    matrix_ref, mine_ref, other_ref, inverse_ref = refs[:4]
    rows_ref, out_ref, window, result, cross, high, low, sems, out_sems = refs[4:]
    col, core, x = where_ref[0], where_ref[1], where_ref[2]
    chunks, long = window.shape[0], window.shape[1]
    rows = long // blocks
    for i in range(chunks):
        fetch(matrix_ref, window.at[i], sems.at[i], i, long).start()
    order = sum([sources(col, hop, n_col) for hop in range(n_col // 2 + 1)], [])
    for piece, chunk in zip(pieces, order):
        high[chunk], low[chunk] = split(load_piece(piece))
    quarters, quarter = mine_ref.shape[0], mine_ref.shape[1]
    for hop in range(quarters):
        spot = lax.rem(x + quarters - hop, quarters)
        base = pl.multiple_of((core * quarters + spot) * quarter, quarter)
        cross[pl.ds(base, quarter)] = mine_ref[hop]
        base = pl.multiple_of(((1 - core) * quarters + spot) * quarter, quarter)
        cross[pl.ds(base, quarter)] = other_ref[hop]
    inverse = inverse_ref[...]
    size = inverse.shape[0]
    every = jnp.concatenate([cross[size * b : size * (b + 1)] for b in range(blocks)], axis=1)
    top = contract(inverse, every, ((1,), (0,)), HIGHEST)
    weights = split(contract(inverse, top, FIRST, HIGHEST))
    for block in range(blocks):
        rows_ref[pl.ds(block, size, stride=blocks), :] = (
            top[:, LANES * block : LANES * (block + 1)] * scale
        )
    high_weights, low_weights = weights

    def write(i):
        start = pl.multiple_of(i * long, long)
        return pltpu.make_async_copy(
            result.at[i], out_ref.at[pl.ds(start, long)], out_sems.at[i]
        )

    def step(i, carry):
        fit = dot3((high[i], low[i]), (high_weights, low_weights), ((1,), (0,)))
        fetch(matrix_ref, window.at[i], sems.at[i], i, long).wait()
        for block in range(blocks):
            result[i, pl.ds(block, rows, stride=blocks), :] = (
                window[i, pl.ds(block, rows, stride=blocks), :]
                - fit[:, LANES * block : LANES * (block + 1)]
            )
        write(i).start()
        return carry

    lax.fori_loop(0, chunks, step, 0)
    for i in range(chunks):
        write(i).wait()


VMEM = pl.BlockSpec(memory_space=pltpu.VMEM)
ANY = pl.BlockSpec(memory_space=pl.ANY)
HBM = pl.BlockSpec(memory_space=pltpu.HBM)
SMEM = pl.BlockSpec(memory_space=pltpu.SMEM)


def pick(value, index):
    return lax.dynamic_index_in_dim(value, index, 0, keepdims=False)


def row_perms(n_row):
    nx = ny = math.isqrt(n_row // 2)

    def rank(x, y, core):
        return (x % nx * ny + y % ny) * 2 + core

    def table(dx, dy, flip):
        return [
            (rank(x, y, core), rank(x + dx, y + dy, core ^ flip))
            for x in range(nx)
            for y in range(ny)
            for core in range(2)
        ]

    return (
        table(0, 0, 1),
        [table(s, 0, 0) for s in range(1, nx)],
        [table(0, s, 0) for s in range(1, ny)],
    )


def send(value, perms):
    return [lax.ppermute(value, "row", perm) for perm in perms]


def total(value, got):
    return (value + got[1]) + (got[0] + got[2])


def hand_out(own, spots, hits, n_col):
    pieces = own.reshape(n_col, -1, LANES)
    first, second = pieces[0], pieces[1]
    for s in range(1, n_col):
        pairs = [(0, s), (1, (1 + s) % n_col)]
        got = lax.ppermute(pick(pieces, spots[s]), "col", pairs)
        first = jnp.where(hits[s], got, first)
        second = jnp.where(hits[(1 + s) % n_col], got, second)
    return jnp.concatenate([first, second])


def after(value, *done):
    return lax.optimization_barrier((value, *done))[0]


def estimate(flops, moved):
    return pl.CostEstimate(flops=flops, bytes_accessed=moved, transcendentals=0)


def per_device(n_row, n_col, matrix):
    rows_here, blocks, _, width = matrix.shape
    col = lax.axis_index("col")
    row = lax.axis_index("row")
    perms = row_perms(n_row)
    nx = len(perms[1]) + 1
    core = lax.rem(row, 2)
    x = row // (n_row // nx)
    where = jnp.stack([col, core, x]).astype(jnp.int32)
    unsigned = jnp.uint32
    spots = [lax.rem(col + s, n_col).astype(unsigned) for s in range(n_col)]
    hits = [col == s for s in range(n_col)]
    steps = [lax.rem(x + s, nx).astype(unsigned) for s in range(nx)]
    this, that = core.astype(unsigned), (1 - core).astype(unsigned)
    matrix, where, spots, hits, steps, this, that = lax.optimization_barrier(
        (matrix, where, spots, hits, steps, this, that)
    )
    flat = matrix.reshape(rows_here * blocks, width)
    size = 2 * width
    rows = rows_here // n_col
    long = rows * blocks
    f32 = jnp.float32
    shape = jax.ShapeDtypeStruct
    flat = pltpu.with_memory_space_constraint(flat, pltpu.HBM)
    cross_shape = shape((blocks, size, width), f32)

    parts = (shape((n_col, rows, blocks * width), jnp.bfloat16),) * 2
    staged = pl.pallas_call(
        functools.partial(stage_kernel, blocks),
        out_shape=parts,
        in_specs=[HBM],
        out_specs=(VMEM, VMEM),
        scratch_shapes=[
            pltpu.VMEM((n_col, long, width), f32),
            pltpu.SemaphoreType.DMA((n_col,)),
        ],
        compiler_params=pltpu.CompilerParams(vmem_limit_bytes=12 << 20),
        cost_estimate=estimate(8 * rows_here * blocks * width, 8 * rows_here * blocks * width),
        name="stage",
    )(flat)

    def collect(hop, pieces, *state):
        shapes = [len(p) for p in pieces]
        return pl.pallas_call(
            functools.partial(collect_kernel, hop, n_col, shapes),
            out_shape=cross_shape,
            in_specs=[SMEM] + [VMEM] * (sum(shapes) + 2 + len(state)),
            out_specs=VMEM,
            compiler_params=pltpu.CompilerParams(vmem_limit_bytes=8 << 20),
            cost_estimate=estimate(
                6 * len(pieces) * rows * size * blocks * width,
                4 * len(pieces) * long * width,
            ),
            name="collect",
        )(where, *sum(pieces, []), *staged, *state)

    def factor(begin, *given):
        start = begin == 0
        return pl.pallas_call(
            functools.partial(factor_kernel, begin, begin + SPAN),
            out_shape=shape((size, size), f32),
            in_specs=[SMEM] + [VMEM] * len(given),
            out_specs=VMEM,
            scratch_shapes=[pltpu.VMEM((3 * width, width), f32)] if start else [],
            compiler_params=pltpu.CompilerParams(vmem_limit_bytes=8 << 20),
            cost_estimate=estimate(256 * size**3, 8 * size * size),
            name="factor",
        )(where, *given)

    up = [(c, (c + 1) % n_col) for c in range(n_col)]
    down = [(c, (c - 1) % n_col) for c in range(n_col)]
    flips = [[(c, c ^ bit) for c in range(n_col)] for bit in (4, 2, 1)]
    swap, along_x, along_y = perms
    piece = hand_out(matrix[:, 0, 0, :], spots, hits, n_col)
    piece, *staged = lax.optimization_barrier((piece, *staged))
    gram = pl.pallas_call(
        gram_kernel,
        out_shape=shape((3, width, width), f32),
        in_specs=[VMEM],
        out_specs=VMEM,
        compiler_params=pltpu.CompilerParams(vmem_limit_bytes=8 << 20),
        cost_estimate=estimate(8 * rows * size * width, 4 * rows * size),
        name="gram",
    )(piece)
    every = [[piece]]

    left, right = lax.ppermute(piece, "col", up), lax.ppermute(piece, "col", down)
    pair = gram.reshape(2, -1, width)
    mine = pick(pair, this) + lax.ppermute(pick(pair, that), "row", swap)
    got = send(mine, along_x)
    cross = collect(0, [[piece]])
    left, right, cross = lax.optimization_barrier((left, right, cross))
    every += [[left], [right]]

    left, right = lax.ppermute(left, "col", up), lax.ppermute(right, "col", down)
    mine = total(mine, got)
    got = send(mine, along_y)
    cross = collect(1, every[1:3], cross)
    left, right, cross, mine = lax.optimization_barrier((left, right, cross, mine))
    every += [[left], [right]]

    left, right = lax.ppermute(left, "col", up), lax.ppermute(right, "col", down)
    mine = total(mine, got)
    got = lax.ppermute(mine, "col", flips[0])
    cross = collect(2, every[3:5], cross)
    left, right, cross, mine = lax.optimization_barrier((left, right, cross, mine))
    every += [[left], [right]]

    last = [
        lax.ppermute(left[:rows], "col", up),
        lax.ppermute(right[rows:], "col", down),
    ]
    mine = mine + got
    got = lax.ppermute(mine, "col", flips[1])
    cross = collect(3, every[5:7], cross)
    *last, cross, mine, got = lax.optimization_barrier((*last, cross, mine, got))
    every += [last]

    mine = mine + got
    got = lax.ppermute(mine, "col", flips[2])
    cross = collect(4, [last], cross)
    whole = cross.reshape(2, nx, -1, width)
    part = pick(whole, this) + lax.ppermute(pick(whole, that), "row", swap)
    took = [
        lax.ppermute(pick(part, steps[s + 1]), "row", p) for s, p in enumerate(along_x)
    ]
    mine = mine + got
    other = lax.ppermute(mine, "row", swap)
    work = factor(0, mine, other)
    part = after(total(pick(part, steps[0]), took), work)
    took = send(part, along_y)
    work = factor(SPAN, work)
    part = after(total(part, took), work)
    took = send(part, along_x)
    work = factor(2 * SPAN, work)
    cross_mine = after(jnp.stack([part, *took]), work)
    cross_other = lax.ppermute(cross_mine, "row", swap)
    work = factor(3 * SPAN, work)
    shapes = [len(p) for p in every]
    scaled, residual = pl.pallas_call(
        functools.partial(
            residual_kernel, n_col, blocks, 1.0 / math.sqrt(rows_here * n_row), shapes
        ),
        out_shape=(
            shape((size * blocks, width), f32),
            shape((rows_here * blocks, width), f32),
        ),
        in_specs=[SMEM] + [VMEM] * sum(shapes) + [HBM, VMEM, VMEM, VMEM],
        out_specs=(VMEM, HBM),
        scratch_shapes=[
            pltpu.VMEM((n_col, long, width), f32),
            pltpu.VMEM((n_col, long, width), f32),
            pltpu.VMEM((size * blocks, width), f32),
            pltpu.VMEM((n_col, rows, size), jnp.bfloat16),
            pltpu.VMEM((n_col, rows, size), jnp.bfloat16),
            pltpu.SemaphoreType.DMA((n_col,)),
            pltpu.SemaphoreType.DMA((n_col,)),
        ],
        compiler_params=pltpu.CompilerParams(vmem_limit_bytes=28 << 20),
        cost_estimate=estimate(
            6 * rows_here * size * blocks * width, 4 * rows_here * (size + 2 * blocks * width)
        ),
        name="residual",
    )(where, *sum(every, []), flat, cross_mine, cross_other, work)
    return (
        scaled.reshape(size, blocks, 1, width),
        residual.reshape(rows_here, blocks, 1, width),
    )


def solution(mesh):
    return jax.shard_map(
        functools.partial(per_device, mesh.shape["row"], mesh.shape["col"]),
        mesh=mesh,
        in_specs=(P("row", None, "col", None),),
        out_specs=(P(None, None, "col", None), P("row", None, "col", None)),
        check_vma=False,
    )
```

profile of v0, /device:TPU:1, one launch (start us, length us, event | category | flops | bytes accessed | tf_op | source)
XLA Modules:
  0.0 124.6 jit_solution(4620607833123618785)
XLA Ops:
  2.1 4.4 %collective-permute-start.6 = (f32[256,128]{1,0:T(8,128)S(1)}, f32[256,128]{1,0:T(8,128)S(1)}, u32[]{:S(2)}, u32[]{:S(2)}) collective-permute-start(f32[256,128]{1,0:T(8,128)S(1)} %get-tuple-element.106), channel_id=1, source_target_pairs={{0,1},{1,2},{8,9},{9,10},{16,17},{17,18},{24,25},{25,26},{32,33},{... | collective-permute-start | bytes 393224 | tf_op jit(solution)/shard_map/ppermute | solution.py:291
  6.5 2.6 %collective-permute-start.5 = (f32[256,128]{1,0:T(8,128)S(1)}, f32[256,128]{1,0:T(8,128)S(1)}, u32[]{:S(2)}, u32[]{:S(2)}) collective-permute-start(f32[256,128]{1,0:T(8,128)S(1)} %get-tuple-element.107), channel_id=1, source_target_pairs={{0,2},{1,3},{8,10},{9,11},{16,18},{17,19},{24,26},{25,27},{32,34},... | collective-permute-start | bytes 393224 | tf_op jit(solution)/shard_map/ppermute | solution.py:291
  11.2 3.2 %collective-permute-start.3 = (f32[256,128]{1,0:T(8,128)S(1)}, f32[256,128]{1,0:T(8,128)S(1)}, u32[]{:S(2)}, u32[]{:S(2)}) collective-permute-start(f32[256,128]{1,0:T(8,128)S(1)} %get-tuple-element.109), channel_id=1, source_target_pairs={{0,4},{1,5},{8,12},{9,13},{16,20},{17,21},{24,28},{25,29},{32,36},... | collective-permute-start | bytes 393224 | tf_op jit(solution)/shard_map/ppermute | solution.py:291
  19.0 2.8 %copy.7 = f32[2048,5,1,128]{3,0,2,1:T(8,128)S(1)} copy(f32[2048,5,1,128]{3,2,1,0:T(1,128)} %param.1) | data formatting | bytes 10485760 | tf_op jit(solution)/shard_map/optimization_barrier | solution.py:319
  21.8 2.7 %stage.1 = (bf16[8,256,640]{2,1,0:T(8,128)(2,1)S(1)}, bf16[8,256,640]{2,1,0:T(8,128)(2,1)S(1)}) custom-call(f32[10240,128]{1,0:T(8,128)} %bitcast.81), custom_call_target="tpu_custom_call" | custom-call | flops 10485760 | bytes 10485760 | tf_op jit(solution)/shard_map/stage/pallas_call | solution.py:332
  25.9 3.0 %collective-permute-done.1 = f32[256,128]{1,0:T(8,128)S(1)} collective-permute-done((f32[256,128]{1,0:T(8,128)S(1)}, f32[256,128]{1,0:T(8,128)S(1)}, u32[]{:S(2)}, u32[]{:S(2)}) %collective-permute-start.1) | collective-permute-done | bytes 131104 | tf_op jit(solution)/shard_map/ppermute | solution.py:291
  28.9 2.8 %collective-permute-done = f32[256,128]{1,0:T(8,128)S(1)} collective-permute-done((f32[256,128]{1,0:T(8,128)S(1)}, f32[256,128]{1,0:T(8,128)S(1)}, u32[]{:S(2)}, u32[]{:S(2)}) %collective-permute-start) | collective-permute-done | bytes 131104 | tf_op jit(solution)/shard_map/ppermute | solution.py:291
  32.8 3.4 %collective-permute-start.8 = (f32[512,128]{1,0:T(8,128)S(1)}, f32[512,128]{1,0:T(8,128)S(1)}, u32[]{:S(2)}, u32[]{:S(2)}) collective-permute-start(f32[512,128]{1,0:T(8,128)S(1)} %pad_maximum_fusion.1.refs_0_.piece_ref), channel_id=1, source_target_pairs={{0,7},{1,0},{2,1},{3,2},{4,3},{5,4},{6,5},{7,6},{8,15},{9,8},{10,9... | collective-permute-start | bytes 786440 | tf_op jit(solution)/shard_map/ppermute | solution.py:391
  36.2 2.6 %collective-permute-start.14 = (f32[192,128]{1,0:T(8,128)S(1)}, f32[192,128]{1,0:T(8,128)S(1)}, u32[]{:S(2)}, u32[]{:S(2)}) collective-permute-start(f32[192,128]{1,0:T(8,128)S(1)} %bitcast_add_fusion.1), channel_id=1, source_target_pairs={{0,192},{8,200},{16,208},{24,216},{32,224},{40,232},{48,240},{56,2... | collective-permute-start | bytes 294920 | tf_op jit(solution)/shard_map/ppermute | solution.py:279
  41.9 3.1 %collective-permute-done.7.refs_0_.refs_1_ = f32[512,128]{1,0:T(8,128)S(1)} collective-permute-done((f32[512,128]{1,0:T(8,128)S(1)}, f32[512,128]{1,0:T(8,128)S(1)}, u32[]{:S(2)}, u32[]{:S(2)}) %collective-permute-start.7) | collective-permute-done | bytes 262176 | tf_op jit(solution)/shard_map/ppermute | solution.py:391
  45.0 2.7 %collective-permute-start.10 = (f32[512,128]{1,0:T(8,128)S(1)}, f32[512,128]{1,0:T(8,128)S(1)}, u32[]{:S(2)}, u32[]{:S(2)}) collective-permute-start(f32[512,128]{1,0:T(8,128)S(1)} %collective-permute-done.8.refs_1_.refs_2_), channel_id=1, source_target_pairs={{0,7},{1,0},{2,1},{3,2},{4,3},{5,4},{6,5},{7,6},{8,15},{9,8},{10,9... | collective-permute-start | bytes 786440 | tf_op jit(solution)/shard_map/ppermute | solution.py:399
  47.7 2.8 %collective-permute-start.19 = (f32[192,128]{1,0:T(8,128)S(1)}, f32[192,128]{1,0:T(8,128)S(1)}, u32[]{:S(2)}, u32[]{:S(2)}) collective-permute-start(f32[192,128]{1,0:T(8,128)S(1)} %add_add_fusion.1), channel_id=1, source_target_pairs={{0,48},{8,56},{16,0},{24,8},{32,16},{40,24},{48,32},{56,40},{64,11... | collective-permute-start | bytes 294920 | tf_op jit(solution)/shard_map/ppermute | solution.py:279
  53.8 2.7 %collective-permute-start.16 = (f32[512,128]{1,0:T(8,128)S(1)}, f32[512,128]{1,0:T(8,128)S(1)}, u32[]{:S(2)}, u32[]{:S(2)}) collective-permute-start(f32[512,128]{1,0:T(8,128)S(1)} %collective-permute-done.10.refs_1_.refs_4_), channel_id=1, source_target_pairs={{0,7},{1,0},{2,1},{3,2},{4,3},{5,4},{6,5},{7,6},{8,15},{9,8},{10,9... | collective-permute-start | bytes 786440 | tf_op jit(solution)/shard_map/ppermute | solution.py:406
  62.3 3.6 %collective-permute-start.21 = (f32[256,128]{1,0:T(8,128)S(1)}, f32[256,128]{1,0:T(8,128)S(1)}, u32[]{:S(2)}, u32[]{:S(2)}) collective-permute-start(f32[256,128]{1,0:T(8,128)S(1)} %slice.23), channel_id=1, source_target_pairs={{0,7},{1,0},{2,1},{3,2},{4,3},{5,4},{6,5},{7,6},{8,15},{9,8},{10,9... | collective-permute-start | bytes 393224 | tf_op jit(solution)/shard_map/ppermute | solution.py:415
  67.4 3.5 %collective-permute-done.23 = f32[192,128]{1,0:T(8,128)S(1)} collective-permute-done((f32[192,128]{1,0:T(8,128)S(1)}, f32[192,128]{1,0:T(8,128)S(1)}, u32[]{:S(2)}, u32[]{:S(2)}) %collective-permute-start.23) | collective-permute-done | bytes 98336 | tf_op jit(solution)/shard_map/ppermute | solution.py:418
  72.1 6.6 %collective-permute-start.24 = (f32[4,160,128]{2,1,0:T(8,128)S(1)}, f32[4,160,128]{2,1,0:T(8,128)S(1)}, u32[]{:S(2)}, u32[]{:S(2)}) collective-permute-start(f32[4,160,128]{2,1,0:T(8,128)S(1)} %dynamic-slice_bitcast_fusion), channel_id=1, source_target_pairs={{0,8},{8,0},{16,24},{24,16},{32,40},{40,32},{48,56},{56,48},{64,72... | collective-permute-start | bytes 983048 | tf_op jit(solution)/shard_map/ppermute | solution.py:427
  78.8 4.4 %collective-permute-done.28 = f32[192,128]{1,0:T(8,128)S(1)} collective-permute-done((f32[192,128]{1,0:T(8,128)S(1)}, f32[192,128]{1,0:T(8,128)S(1)}, u32[]{:S(2)}, u32[]{:S(2)}) %collective-permute-start.28) | collective-permute-done | bytes 98336 | tf_op jit(solution)/shard_map/ppermute | solution.py:424
  84.1 2.6 %collective-permute-start.27 = (f32[160,128]{1,0:T(8,128)S(1)}, f32[160,128]{1,0:T(8,128)S(1)}, u32[]{:S(2)}, u32[]{:S(2)}) collective-permute-start(f32[160,128]{1,0:T(8,128)S(1)} %get-tuple-element.113), channel_id=1, source_target_pairs={{0,192},{8,200},{16,208},{24,216},{32,224},{40,232},{48,240},{56,2... | collective-permute-start | bytes 245768 | tf_op jit(solution)/shard_map/ppermute | solution.py:429
  88.4 4.2 %factor.4.refs_0_ = f32[256,256]{1,0:T(8,128)S(1)} custom-call(s32[3]{0:T(128)S(1)} %pad_add_fusion.where_ref, f32[192,128]{1,0:T(8,128)S(1)} %add.105.refs_0_, f32[192,128]{1,0:T(8,128)S(1)} %collective-permute-done.29.refs_1_), custom_call_target="tpu_custom_call" | custom-call | flops 4294967296 | bytes 524288 | tf_op jit(solution)/shard_map/factor/pallas_call | solution.py:363
  97.3 3.9 %factor.5.refs_0_ = f32[256,256]{1,0:T(8,128)S(1)} custom-call(s32[3]{0:T(128)S(1)} %pad_add_fusion.where_ref, f32[256,256]{1,0:T(8,128)S(1)} %factor.4.refs_0_), custom_call_target="tpu_custom_call" | custom-call | flops 4294967296 | bytes 524288 | tf_op jit(solution)/shard_map/factor/pallas_call | solution.py:363
  103.8 3.8 %factor.6.refs_0_ = f32[256,256]{1,0:T(8,128)S(1)} custom-call(s32[3]{0:T(128)S(1)} %pad_add_fusion.where_ref, f32[256,256]{1,0:T(8,128)S(1)} %factor.5.refs_0_), custom_call_target="tpu_custom_call" | custom-call | flops 4294967296 | bytes 524288 | tf_op jit(solution)/shard_map/factor/pallas_call | solution.py:363
  108.3 4.0 %collective-permute-start.36 = (f32[4,160,128]{2,1,0:T(8,128)S(1)}, f32[4,160,128]{2,1,0:T(8,128)S(1)}, u32[]{:S(2)}, u32[]{:S(2)}) collective-permute-start(f32[4,160,128]{2,1,0:T(8,128)S(1)} %pad_maximum_fusion.refs_10_), channel_id=1, source_target_pairs={{0,8},{8,0},{16,24},{24,16},{32,40},{40,32},{48,56},{56,48},{64,72... | collective-permute-start | bytes 983048 | tf_op jit(solution)/shard_map/ppermute | solution.py:441
  112.3 3.4 %factor.7.refs_12_ = f32[256,256]{1,0:T(8,128)S(1)} custom-call(s32[3]{0:T(128)S(1)} %pad_add_fusion.where_ref, f32[256,256]{1,0:T(8,128)S(1)} %factor.6.refs_0_), custom_call_target="tpu_custom_call" | custom-call | flops 4294967296 | bytes 524288 | tf_op jit(solution)/shard_map/factor/pallas_call | solution.py:363
  115.7 8.7 %residual.1 = (f32[1280,128]{1,0:T(8,128)}, f32[10240,128]{1,0:T(8,128)}) custom-call(s32[3]{0:T(128)S(1)} %pad_add_fusion.where_ref, f32[512,128]{1,0:T(8,128)S(1)} %pad_maximum_fusion.1.refs_0_.piece_ref, f32[512,128]{1,0:T(8,128)S(1)} %collective-permute-done.7.refs_0_.refs_1_, f32[512,128]{1,0:T(8,128)S(1)} %collective-permute-done.8.refs_1_.refs_2_, ...), custom_call_target="tpu_custom_call" | custom-call | flops 2013265920 | bytes 12582912 | tf_op jit(solution)/shard_map/residual/pallas_call | solution.py:444
  (83 shorter events, 35.9 us)
Async XLA Ops:
  2.1 13.6 %collective-permute-start.6 = (f32[256,128]{1,0:T(8,128)S(1)}, f32[256,128]{1,0:T(8,128)S(1)}, u32[]{:S(2)}, u32[]{:S(2)}) collective-permute-start(f32[256,128]{1,0:T(8,128)S(1)} %get-tuple-element.106), channel_id=1, source_target_pairs={{0,1},{1,2},{8,9},{9,10},{16,17},{17,18},{24,25},{25,26},{32,33},{... | collective-permute-start | bytes 393224 | tf_op jit(solution)/shard_map/ppermute | solution.py:291
  6.5 10.5 %collective-permute-start.5 = (f32[256,128]{1,0:T(8,128)S(1)}, f32[256,128]{1,0:T(8,128)S(1)}, u32[]{:S(2)}, u32[]{:S(2)}) collective-permute-start(f32[256,128]{1,0:T(8,128)S(1)} %get-tuple-element.107), channel_id=1, source_target_pairs={{0,2},{1,3},{8,10},{9,11},{16,18},{17,19},{24,26},{25,27},{32,34},... | collective-permute-start | bytes 393224 | tf_op jit(solution)/shard_map/ppermute | solution.py:291
  9.2 15.3 %collective-permute-start.4 = (f32[256,128]{1,0:T(8,128)S(1)}, f32[256,128]{1,0:T(8,128)S(1)}, u32[]{:S(2)}, u32[]{:S(2)}) collective-permute-start(f32[256,128]{1,0:T(8,128)S(1)} %get-tuple-element.108), channel_id=1, source_target_pairs={{0,3},{1,4},{8,11},{9,12},{16,19},{17,20},{24,27},{25,28},{32,35},... | collective-permute-start | bytes 393224 | tf_op jit(solution)/shard_map/ppermute | solution.py:291
  11.2 13.3 %collective-permute-start.3 = (f32[256,128]{1,0:T(8,128)S(1)}, f32[256,128]{1,0:T(8,128)S(1)}, u32[]{:S(2)}, u32[]{:S(2)}) collective-permute-start(f32[256,128]{1,0:T(8,128)S(1)} %get-tuple-element.109), channel_id=1, source_target_pairs={{0,4},{1,5},{8,12},{9,13},{16,20},{17,21},{24,28},{25,29},{32,36},... | collective-permute-start | bytes 393224 | tf_op jit(solution)/shard_map/ppermute | solution.py:291
  14.4 11.5 %collective-permute-start.2 = (f32[256,128]{1,0:T(8,128)S(1)}, f32[256,128]{1,0:T(8,128)S(1)}, u32[]{:S(2)}, u32[]{:S(2)}) collective-permute-start(f32[256,128]{1,0:T(8,128)S(1)} %get-tuple-element.110), channel_id=1, source_target_pairs={{0,5},{1,6},{8,13},{9,14},{16,21},{17,22},{24,29},{25,30},{32,37},... | collective-permute-start | bytes 393224 | tf_op jit(solution)/shard_map/ppermute | solution.py:291
  15.8 13.1 %collective-permute-start.1 = (f32[256,128]{1,0:T(8,128)S(1)}, f32[256,128]{1,0:T(8,128)S(1)}, u32[]{:S(2)}, u32[]{:S(2)}) collective-permute-start(f32[256,128]{1,0:T(8,128)S(1)} %get-tuple-element.111), channel_id=1, source_target_pairs={{0,6},{1,7},{8,14},{9,15},{16,22},{17,23},{24,30},{25,31},{32,38},... | collective-permute-start | bytes 393224 | tf_op jit(solution)/shard_map/ppermute | solution.py:291
  17.1 14.6 %collective-permute-start = (f32[256,128]{1,0:T(8,128)S(1)}, f32[256,128]{1,0:T(8,128)S(1)}, u32[]{:S(2)}, u32[]{:S(2)}) collective-permute-start(f32[256,128]{1,0:T(8,128)S(1)} %get-tuple-element.112), channel_id=1, source_target_pairs={{0,7},{1,0},{8,15},{9,8},{16,23},{17,16},{24,31},{25,24},{32,39},{... | collective-permute-start | bytes 393224 | tf_op jit(solution)/shard_map/ppermute | solution.py:291
  32.8 9.1 %collective-permute-start.8 = (f32[512,128]{1,0:T(8,128)S(1)}, f32[512,128]{1,0:T(8,128)S(1)}, u32[]{:S(2)}, u32[]{:S(2)}) collective-permute-start(f32[512,128]{1,0:T(8,128)S(1)} %pad_maximum_fusion.1.refs_0_.piece_ref), channel_id=1, source_target_pairs={{0,7},{1,0},{2,1},{3,2},{4,3},{5,4},{6,5},{7,6},{8,15},{9,8},{10,9... | collective-permute-start | bytes 786440 | tf_op jit(solution)/shard_map/ppermute | solution.py:391
  36.2 8.7 %collective-permute-start.7 = (f32[512,128]{1,0:T(8,128)S(1)}, f32[512,128]{1,0:T(8,128)S(1)}, u32[]{:S(2)}, u32[]{:S(2)}) collective-permute-start(f32[512,128]{1,0:T(8,128)S(1)} %pad_maximum_fusion.1.refs_0_.piece_ref), channel_id=1, source_target_pairs={{0,1},{1,2},{2,3},{3,4},{4,5},{5,6},{6,7},{7,0},{8,9},{9,10},{10,1... | collective-permute-start | bytes 786440 | tf_op jit(solution)/shard_map/ppermute | solution.py:391
  36.2 11.4 %collective-permute-start.14 = (f32[192,128]{1,0:T(8,128)S(1)}, f32[192,128]{1,0:T(8,128)S(1)}, u32[]{:S(2)}, u32[]{:S(2)}) collective-permute-start(f32[192,128]{1,0:T(8,128)S(1)} %bitcast_add_fusion.1), channel_id=1, source_target_pairs={{0,192},{8,200},{16,208},{24,216},{32,224},{40,232},{48,240},{56,2... | collective-permute-start | bytes 294920 | tf_op jit(solution)/shard_map/ppermute | solution.py:279
  38.8 8.8 %collective-permute-start.13 = (f32[192,128]{1,0:T(8,128)S(1)}, f32[192,128]{1,0:T(8,128)S(1)}, u32[]{:S(2)}, u32[]{:S(2)}) collective-permute-start(f32[192,128]{1,0:T(8,128)S(1)} %bitcast_add_fusion.1), channel_id=1, source_target_pairs={{0,64},{8,72},{16,80},{24,88},{32,96},{40,104},{48,112},{56,120},{... | collective-permute-start | bytes 294920 | tf_op jit(solution)/shard_map/ppermute | solution.py:279
  38.8 8.8 %collective-permute-start.12 = (f32[192,128]{1,0:T(8,128)S(1)}, f32[192,128]{1,0:T(8,128)S(1)}, u32[]{:S(2)}, u32[]{:S(2)}) collective-permute-start(f32[192,128]{1,0:T(8,128)S(1)} %bitcast_add_fusion.1), channel_id=1, source_target_pairs={{0,128},{8,136},{16,144},{24,152},{32,160},{40,168},{48,176},{56,1... | collective-permute-start | bytes 294920 | tf_op jit(solution)/shard_map/ppermute | solution.py:279
  45.0 8.5 %collective-permute-start.9 = (f32[512,128]{1,0:T(8,128)S(1)}, f32[512,128]{1,0:T(8,128)S(1)}, u32[]{:S(2)}, u32[]{:S(2)}) collective-permute-start(f32[512,128]{1,0:T(8,128)S(1)} %collective-permute-done.7.refs_0_.refs_1_), channel_id=1, source_target_pairs={{0,1},{1,2},{2,3},{3,4},{4,5},{5,6},{6,7},{7,0},{8,9},{9,10},{10,1... | collective-permute-start | bytes 786440 | tf_op jit(solution)/shard_map/ppermute | solution.py:399
  45.0 8.5 %collective-permute-start.10 = (f32[512,128]{1,0:T(8,128)S(1)}, f32[512,128]{1,0:T(8,128)S(1)}, u32[]{:S(2)}, u32[]{:S(2)}) collective-permute-start(f32[512,128]{1,0:T(8,128)S(1)} %collective-permute-done.8.refs_1_.refs_2_), channel_id=1, source_target_pairs={{0,7},{1,0},{2,1},{3,2},{4,3},{5,4},{6,5},{7,6},{8,15},{9,8},{10,9... | collective-permute-start | bytes 786440 | tf_op jit(solution)/shard_map/ppermute | solution.py:399
  47.7 8.8 %collective-permute-start.19 = (f32[192,128]{1,0:T(8,128)S(1)}, f32[192,128]{1,0:T(8,128)S(1)}, u32[]{:S(2)}, u32[]{:S(2)}) collective-permute-start(f32[192,128]{1,0:T(8,128)S(1)} %add_add_fusion.1), channel_id=1, source_target_pairs={{0,48},{8,56},{16,0},{24,8},{32,16},{40,24},{48,32},{56,40},{64,11... | collective-permute-start | bytes 294920 | tf_op jit(solution)/shard_map/ppermute | solution.py:279
  53.8 8.5 %collective-permute-start.16 = (f32[512,128]{1,0:T(8,128)S(1)}, f32[512,128]{1,0:T(8,128)S(1)}, u32[]{:S(2)}, u32[]{:S(2)}) collective-permute-start(f32[512,128]{1,0:T(8,128)S(1)} %collective-permute-done.10.refs_1_.refs_4_), channel_id=1, source_target_pairs={{0,7},{1,0},{2,1},{3,2},{4,3},{5,4},{6,5},{7,6},{8,15},{9,8},{10,9... | collective-permute-start | bytes 786440 | tf_op jit(solution)/shard_map/ppermute | solution.py:406
  56.5 9.4 %collective-permute-start.22 = (f32[192,128]{1,0:T(8,128)S(1)}, f32[192,128]{1,0:T(8,128)S(1)}, u32[]{:S(2)}, u32[]{:S(2)}) collective-permute-start(f32[192,128]{1,0:T(8,128)S(1)} %add_add_fusion), channel_id=1, source_target_pairs={{0,4},{1,5},{2,6},{3,7},{4,0},{5,1},{6,2},{7,3},{8,12},{9,13},{10,... | collective-permute-start | bytes 294920 | tf_op jit(solution)/shard_map/ppermute | solution.py:408
  62.3 8.6 %collective-permute-start.21 = (f32[256,128]{1,0:T(8,128)S(1)}, f32[256,128]{1,0:T(8,128)S(1)}, u32[]{:S(2)}, u32[]{:S(2)}) collective-permute-start(f32[256,128]{1,0:T(8,128)S(1)} %slice.23), channel_id=1, source_target_pairs={{0,7},{1,0},{2,1},{3,2},{4,3},{5,4},{6,5},{7,6},{8,15},{9,8},{10,9... | collective-permute-start | bytes 393224 | tf_op jit(solution)/shard_map/ppermute | solution.py:415
  72.1 12.0 %collective-permute-start.24 = (f32[4,160,128]{2,1,0:T(8,128)S(1)}, f32[4,160,128]{2,1,0:T(8,128)S(1)}, u32[]{:S(2)}, u32[]{:S(2)}) collective-permute-start(f32[4,160,128]{2,1,0:T(8,128)S(1)} %dynamic-slice_bitcast_fusion), channel_id=1, source_target_pairs={{0,8},{8,0},{16,24},{24,16},{32,40},{40,32},{48,56},{56,48},{64,72... | collective-permute-start | bytes 983048 | tf_op jit(solution)/shard_map/ppermute | solution.py:427
  84.1 8.5 %collective-permute-start.27 = (f32[160,128]{1,0:T(8,128)S(1)}, f32[160,128]{1,0:T(8,128)S(1)}, u32[]{:S(2)}, u32[]{:S(2)}) collective-permute-start(f32[160,128]{1,0:T(8,128)S(1)} %get-tuple-element.113), channel_id=1, source_target_pairs={{0,192},{8,200},{16,208},{24,216},{32,224},{40,232},{48,240},{56,2... | collective-permute-start | bytes 245768 | tf_op jit(solution)/shard_map/ppermute | solution.py:429
  86.7 7.0 %collective-permute-start.26 = (f32[160,128]{1,0:T(8,128)S(1)}, f32[160,128]{1,0:T(8,128)S(1)}, u32[]{:S(2)}, u32[]{:S(2)}) collective-permute-start(f32[160,128]{1,0:T(8,128)S(1)} %get-tuple-element.114), channel_id=1, source_target_pairs={{0,64},{8,72},{16,80},{24,88},{32,96},{40,104},{48,112},{56,120},{... | collective-permute-start | bytes 245768 | tf_op jit(solution)/shard_map/ppermute | solution.py:429
  86.7 7.0 %collective-permute-start.25 = (f32[160,128]{1,0:T(8,128)S(1)}, f32[160,128]{1,0:T(8,128)S(1)}, u32[]{:S(2)}, u32[]{:S(2)}) collective-permute-start(f32[160,128]{1,0:T(8,128)S(1)} %get-tuple-element.115), channel_id=1, source_target_pairs={{0,128},{8,136},{16,144},{24,152},{32,160},{40,168},{48,176},{56,1... | collective-permute-start | bytes 245768 | tf_op jit(solution)/shard_map/ppermute | solution.py:429
  93.7 7.6 %collective-permute-start.32 = (f32[160,128]{1,0:T(8,128)S(1)}, f32[160,128]{1,0:T(8,128)S(1)}, u32[]{:S(2)}, u32[]{:S(2)}) collective-permute-start(f32[160,128]{1,0:T(8,128)S(1)} %fusion.14), channel_id=1, source_target_pairs={{0,48},{8,56},{16,0},{24,8},{32,16},{40,24},{48,32},{56,40},{64,11... | collective-permute-start | bytes 245768 | tf_op jit(solution)/shard_map/ppermute | solution.py:279
  108.3 7.4 %collective-permute-start.36 = (f32[4,160,128]{2,1,0:T(8,128)S(1)}, f32[4,160,128]{2,1,0:T(8,128)S(1)}, u32[]{:S(2)}, u32[]{:S(2)}) collective-permute-start(f32[4,160,128]{2,1,0:T(8,128)S(1)} %pad_maximum_fusion.refs_10_), channel_id=1, source_target_pairs={{0,8},{8,0},{16,24},{24,16},{32,40},{40,32},{48,56},{56,48},{64,72... | collective-permute-start | bytes 983048 | tf_op jit(solution)/shard_map/ppermute | solution.py:441
  (13 other events, 70.0 us)
where the time goes:
time: 125 us
  starting transfers between devices  60.9 us (49%)
  Pallas kernels  33.3 us (27%)
  waiting for transfers between devices  24.5 us (20%)
  local copies, waits for them, and re-layouts  4.25 us (3%)
  between operations  1.29 us (1%)
    ppermute x7, starting transfers between devices, hand_out(): got = lax.ppermute(pick(pieces, spots[s]), 'col', pairs)  16.8 us
    pallas_call x4, Pallas kernels, factor(): pl.pallas_call(functools.partial(factor_kernel, begin, begin + SPAN), out...  15.4 us
    ppermute x12, starting transfers between devices, send(): return [lax.ppermute(value, 'row', perm) for perm in perms]  14.8 us
    pallas_call x1, Pallas kernels, per_device(): pl.pallas_call(functools.partial(residual_kernel, n_col, blocks, 1.0 / ma...  8.68 us
    ppermute x7, waiting for transfers between devices, hand_out(): got = lax.ppermute(pick(pieces, spots[s]), 'col', pairs)  7.18 us
    ppermute x1, starting transfers between devices, per_device(): part = pick(whole, this) + lax.ppermute(pick(whole, that), 'row', swap)  6.56 us
    pallas_call x5, Pallas kernels, collect(): pl.pallas_call(functools.partial(collect_kernel, hop, n_col, shapes), out...  6.18 us
    ppermute x2, starting transfers between devices, per_device(): lax.ppermute(right, 'col', down)  5.34 us
  transfers between devices with their start and end apart: 37, of which 12 were waited for; matrix products, arithmetic and copies ran while one was open for 2% of the time, Pallas kernels for 19%

commit v1 on v0

--- a/solution.py
+++ b/solution.py
@@ -104,10 +104,13 @@
 def factor_kernel(begin, end, where_ref, *refs):
     if begin == 0:
         mine_ref, other_ref, work, parts = refs
-        core = where_ref[1]
-        count = mine_ref.shape[0]
-        parts[pl.ds(pl.multiple_of(core * count, count), count)] = mine_ref[...]
-        parts[pl.ds(pl.multiple_of((1 - core) * count, count), count)] = other_ref[...]
+        core, x = where_ref[1], where_ref[2]
+        quarters, count = mine_ref.shape[0], mine_ref.shape[1]
+        for hop in range(quarters):
+            spot = lax.rem(x + quarters - hop, quarters)
+            for side, ref in ((core, mine_ref), (1 - core, other_ref)):
+                base = pl.multiple_of((side * quarters + spot) * count, count)
+                parts[pl.ds(base, count)] = ref[hop]
         work[:LANES, :LANES] = parts[:LANES]
         work[:LANES, LANES:] = parts[2 * LANES :]
         work[LANES:, :LANES] = jnp.zeros((LANES, LANES), jnp.float32)
@@ -196,7 +199,7 @@
         refs = refs[count:]
     matrix_ref, mine_ref, other_ref, inverse_ref = refs[:4]
     rows_ref, out_ref, window, result, cross, high, low, sems, out_sems = refs[4:]
-    col, core, x = where_ref[0], where_ref[1], where_ref[2]
+    col, core = where_ref[0], where_ref[1]
     chunks, long = window.shape[0], window.shape[1]
     rows = long // blocks
     for i in range(chunks):
@@ -204,13 +207,9 @@
     order = sum([sources(col, hop, n_col) for hop in range(n_col // 2 + 1)], [])
     for piece, chunk in zip(pieces, order):
         high[chunk], low[chunk] = split(load_piece(piece))
-    quarters, quarter = mine_ref.shape[0], mine_ref.shape[1]
-    for hop in range(quarters):
-        spot = lax.rem(x + quarters - hop, quarters)
-        base = pl.multiple_of((core * quarters + spot) * quarter, quarter)
-        cross[pl.ds(base, quarter)] = mine_ref[hop]
-        base = pl.multiple_of(((1 - core) * quarters + spot) * quarter, quarter)
-        cross[pl.ds(base, quarter)] = other_ref[hop]
+    count = mine_ref.shape[0]
+    cross[pl.ds(pl.multiple_of(core * count, count), count)] = mine_ref[...]
+    cross[pl.ds(pl.multiple_of((1 - core) * count, count), count)] = other_ref[...]
     inverse = inverse_ref[...]
     size = inverse.shape[0]
     every = jnp.concatenate([cross[size * b : size * (b + 1)] for b in range(blocks)], axis=1)
@@ -272,11 +271,16 @@
         table(0, 0, 1),
         [table(s, 0, 0) for s in range(1, nx)],
         [table(0, s, 0) for s in range(1, ny)],
+        [[rank(x, y, core) for x in range(nx) for y in range(ny)] for core in range(2)],
     )
 
 
 def send(value, perms):
     return [lax.ppermute(value, "row", perm) for perm in perms]
+
+
+def exchange(value, groups):
+    return lax.all_to_all(value, "row", 0, 0, axis_index_groups=groups)
 
 
 def total(value, got):
@@ -374,7 +378,7 @@
     up = [(c, (c + 1) % n_col) for c in range(n_col)]
     down = [(c, (c - 1) % n_col) for c in range(n_col)]
     flips = [[(c, c ^ bit) for c in range(n_col)] for bit in (4, 2, 1)]
-    swap, along_x, along_y = perms
+    swap, along_x, along_y, chips = perms
     piece = hand_out(matrix[:, 0, 0, :], spots, hits, n_col)
     piece, *staged = lax.optimization_barrier((piece, *staged))
     gram = pl.pallas_call(
@@ -391,13 +395,14 @@
     left, right = lax.ppermute(piece, "col", up), lax.ppermute(piece, "col", down)
     pair = gram.reshape(2, -1, width)
     mine = pick(pair, this) + lax.ppermute(pick(pair, that), "row", swap)
-    got = send(mine, along_x)
+    mine = mine.reshape(nx, -1, width)
+    got = [lax.ppermute(pick(mine, steps[s + 1]), "row", p) for s, p in enumerate(along_x)]
     cross = collect(0, [[piece]])
     left, right, cross = lax.optimization_barrier((left, right, cross))
     every += [[left], [right]]
 
     left, right = lax.ppermute(left, "col", up), lax.ppermute(right, "col", down)
-    mine = total(mine, got)
+    mine = total(pick(mine, steps[0]), got)
     got = send(mine, along_y)
     cross = collect(1, every[1:3], cross)
     left, right, cross, mine = lax.optimization_barrier((left, right, cross, mine))
@@ -405,9 +410,10 @@
 
     left, right = lax.ppermute(left, "col", up), lax.ppermute(right, "col", down)
     mine = total(mine, got)
-    got = lax.ppermute(mine, "col", flips[0])
+    mine = mine + lax.ppermute(mine, "col", flips[0])
+    got = lax.ppermute(mine, "col", flips[1])
     cross = collect(2, every[3:5], cross)
-    left, right, cross, mine = lax.optimization_barrier((left, right, cross, mine))
+    left, right, cross, mine, got = lax.optimization_barrier((left, right, cross, mine, got))
     every += [[left], [right]]
 
     last = [
@@ -415,31 +421,25 @@
         lax.ppermute(right[rows:], "col", down),
     ]
     mine = mine + got
-    got = lax.ppermute(mine, "col", flips[1])
+    mine = mine + lax.ppermute(mine, "col", flips[2])
+    got = send(mine, along_x)
     cross = collect(3, every[5:7], cross)
-    *last, cross, mine, got = lax.optimization_barrier((*last, cross, mine, got))
+    *last, cross, mine = lax.optimization_barrier((*last, cross, mine))
     every += [last]
 
-    mine = mine + got
-    got = lax.ppermute(mine, "col", flips[2])
     cross = collect(4, [last], cross)
-    whole = cross.reshape(2, nx, -1, width)
+    whole = cross.reshape(2, len(chips[0]), -1, width)
     part = pick(whole, this) + lax.ppermute(pick(whole, that), "row", swap)
-    took = [
-        lax.ppermute(pick(part, steps[s + 1]), "row", p) for s, p in enumerate(along_x)
-    ]
-    mine = mine + got
+    took = exchange(part, chips)
+    mine = after(jnp.stack([mine, *got]), part)
     other = lax.ppermute(mine, "row", swap)
-    work = factor(0, mine, other)
-    part = after(total(pick(part, steps[0]), took), work)
-    took = send(part, along_y)
-    work = factor(SPAN, work)
-    part = after(total(part, took), work)
-    took = send(part, along_x)
-    work = factor(2 * SPAN, work)
-    cross_mine = after(jnp.stack([part, *took]), work)
+    work = factor(SPAN, factor(0, mine, other))
+    part = jnp.broadcast_to(jnp.sum(took, axis=0), took.shape)
+    part, work = lax.optimization_barrier((part, work))
+    took = exchange(part, chips)
+    work = factor(3 * SPAN, factor(2 * SPAN, work))
+    cross_mine = after(took.reshape(-1, width), work)
     cross_other = lax.ppermute(cross_mine, "row", swap)
-    work = factor(3 * SPAN, work)
     shapes = [len(p) for p in every]
     scaled, residual = pl.pallas_call(
         functools.partial(

time: 125 us -> 131 us (1.048)
  waiting for transfers between devices: 24.5 us -> 27.7 us
  starting transfers between devices: 60.9 us -> 62.6 us
    all_to_all x0 -> x2, starting transfers between devices: none -> 11.5 us  [exchange(): return lax.all_to_all(value, 'row', 0, 0, axis_index_groups=groups)]
    ppermute x12 -> x6, starting transfers between devices: 14.8 us -> 8.08 us  [send(): return [lax.ppermute(value, 'row', perm) for perm in perms]]
    ppermute x1, starting transfers between devices: 3.63 us -> 0.4 us  [per_device(): lax.ppermute(right[rows:], 'col', down)]
    ppermute x5, waiting for transfers between devices: 5.41 us -> 8.23 us  [the longest x1 6.7 us: per_device(): mine = mine + lax.ppermute(mine, 'col', flips[0])]
    ppermute x12 -> x6, waiting for transfers between devices: 0.66 us -> 3.33 us  [send(): return [lax.ppermute(value, 'row', perm) for perm in perms]]
    ppermute x2, waiting for transfers between devices: 2.26 us -> 0.01 us  [per_device(): lax.ppermute(left, 'col', up)]
    ppermute x2, waiting for transfers between devices: 2.06 us -> 0.01 us  [per_device(): lax.ppermute(right, 'col', down)]
    ppermute x1, starting transfers between devices: 3.99 us -> 2.27 us  [per_device(): cross_other = lax.ppermute(cross_mine, 'row', swap)]
  transfers between devices with their start and end apart: 37 -> 33, of which waited for: 12 -> 14; matrix products, arithmetic and copies ran while one was open for 2% -> 2% of each run, Pallas kernels for 19% -> 18%
where the time goes in v1:
time: 131 us
  starting transfers between devices  62.6 us (48%)
  Pallas kernels  33.3 us (25%)
  waiting for transfers between devices  27.7 us (21%)
  local copies, waits for them, and re-layouts  4.98 us (4%)
    ppermute x7, starting transfers between devices, hand_out(): got = lax.ppermute(pick(pieces, spots[s]), 'col', pairs)  16.8 us
    pallas_call x4, Pallas kernels, factor(): pl.pallas_call(functools.partial(factor_kernel, begin, begin + SPAN), out...  15.4 us
    all_to_all x2, starting transfers between devices, exchange(): return lax.all_to_all(value, 'row', 0, 0, axis_index_groups=groups)  11.5 us
    pallas_call x1, Pallas kernels, per_device(): pl.pallas_call(functools.partial(residual_kernel, n_col, blocks, 1.0 / ma...  8.71 us
    ppermute x6, starting transfers between devices, send(): return [lax.ppermute(value, 'row', perm) for perm in perms]  8.08 us
    ppermute x7, waiting for transfers between devices, hand_out(): got = lax.ppermute(pick(pieces, spots[s]), 'col', pairs)  7.18 us
    ppermute x1, waiting for transfers between devices, per_device(): mine = mine + lax.ppermute(mine, 'col', flips[0])  6.7 us
    ppermute x1, starting transfers between devices, per_device(): part = pick(whole, this) + lax.ppermute(pick(whole, that), 'row', swap)  6.62 us
  transfers between devices with their start and end apart: 33, of which 14 were waited for; matrix products, arithmetic and copies ran while one was open for 2% of the time, Pallas kernels for 18%

profile of v1, /device:TPU:1, one launch (start us, length us, event | category | flops | bytes accessed | tf_op | source)
XLA Modules:
  0.0 130.8 jit_solution(11817556368136296543)
XLA Ops:
  2.1 4.4 %collective-permute-start.6 = (f32[256,128]{1,0:T(8,128)S(1)}, f32[256,128]{1,0:T(8,128)S(1)}, u32[]{:S(2)}, u32[]{:S(2)}) collective-permute-start(f32[256,128]{1,0:T(8,128)S(1)} %get-tuple-element.108), channel_id=1, source_target_pairs={{0,1},{1,2},{8,9},{9,10},{16,17},{17,18},{24,25},{25,26},{32,33},{... | collective-permute-start | bytes 393224 | tf_op jit(solution)/shard_map/ppermute | solution.py:295
  6.5 2.6 %collective-permute-start.5 = (f32[256,128]{1,0:T(8,128)S(1)}, f32[256,128]{1,0:T(8,128)S(1)}, u32[]{:S(2)}, u32[]{:S(2)}) collective-permute-start(f32[256,128]{1,0:T(8,128)S(1)} %get-tuple-element.109), channel_id=1, source_target_pairs={{0,2},{1,3},{8,10},{9,11},{16,18},{17,19},{24,26},{25,27},{32,34},... | collective-permute-start | bytes 393224 | tf_op jit(solution)/shard_map/ppermute | solution.py:295
  11.2 3.2 %collective-permute-start.3 = (f32[256,128]{1,0:T(8,128)S(1)}, f32[256,128]{1,0:T(8,128)S(1)}, u32[]{:S(2)}, u32[]{:S(2)}) collective-permute-start(f32[256,128]{1,0:T(8,128)S(1)} %get-tuple-element.111), channel_id=1, source_target_pairs={{0,4},{1,5},{8,12},{9,13},{16,20},{17,21},{24,28},{25,29},{32,36},... | collective-permute-start | bytes 393224 | tf_op jit(solution)/shard_map/ppermute | solution.py:295
  19.0 2.8 %copy.7 = f32[2048,5,1,128]{3,0,2,1:T(8,128)S(1)} copy(f32[2048,5,1,128]{3,2,1,0:T(1,128)} %param.1) | data formatting | bytes 10485760 | tf_op jit(solution)/shard_map/optimization_barrier | solution.py:323
  21.8 2.7 %stage.1 = (bf16[8,256,640]{2,1,0:T(8,128)(2,1)S(1)}, bf16[8,256,640]{2,1,0:T(8,128)(2,1)S(1)}) custom-call(f32[10240,128]{1,0:T(8,128)} %bitcast.85), custom_call_target="tpu_custom_call" | custom-call | flops 10485760 | bytes 10485760 | tf_op jit(solution)/shard_map/stage/pallas_call | solution.py:336
  25.9 3.0 %collective-permute-done.1 = f32[256,128]{1,0:T(8,128)S(1)} collective-permute-done((f32[256,128]{1,0:T(8,128)S(1)}, f32[256,128]{1,0:T(8,128)S(1)}, u32[]{:S(2)}, u32[]{:S(2)}) %collective-permute-start.1) | collective-permute-done | bytes 131104 | tf_op jit(solution)/shard_map/ppermute | solution.py:295
  28.9 2.8 %collective-permute-done = f32[256,128]{1,0:T(8,128)S(1)} collective-permute-done((f32[256,128]{1,0:T(8,128)S(1)}, f32[256,128]{1,0:T(8,128)S(1)}, u32[]{:S(2)}, u32[]{:S(2)}) %collective-permute-start) | collective-permute-done | bytes 131104 | tf_op jit(solution)/shard_map/ppermute | solution.py:295
  32.8 3.4 %collective-permute-start.8 = (f32[512,128]{1,0:T(8,128)S(1)}, f32[512,128]{1,0:T(8,128)S(1)}, u32[]{:S(2)}, u32[]{:S(2)}) collective-permute-start(f32[512,128]{1,0:T(8,128)S(1)} %pad_maximum_fusion.refs_0_.piece_ref), channel_id=1, source_target_pairs={{0,7},{1,0},{2,1},{3,2},{4,3},{5,4},{6,5},{7,6},{8,15},{9,8},{10,9... | collective-permute-start | bytes 786440 | tf_op jit(solution)/shard_map/ppermute | solution.py:395
  36.3 2.6 %collective-permute-start.14 = (f32[48,128]{1,0:T(8,128)S(1)}, f32[48,128]{1,0:T(8,128)S(1)}, u32[]{:S(2)}, u32[]{:S(2)}) collective-permute-start(f32[48,128]{1,0:T(8,128)S(1)} %get-tuple-element.115), channel_id=1, source_target_pairs={{0,192},{8,200},{16,208},{24,216},{32,224},{40,232},{48,240},{56,2... | collective-permute-start | bytes 73736 | tf_op jit(solution)/shard_map/ppermute | solution.py:399
  41.9 3.1 %collective-permute-done.7.refs_0_.refs_1_ = f32[512,128]{1,0:T(8,128)S(1)} collective-permute-done((f32[512,128]{1,0:T(8,128)S(1)}, f32[512,128]{1,0:T(8,128)S(1)}, u32[]{:S(2)}, u32[]{:S(2)}) %collective-permute-start.7) | collective-permute-done | bytes 262176 | tf_op jit(solution)/shard_map/ppermute | solution.py:395
  45.0 2.7 %collective-permute-start.10 = (f32[512,128]{1,0:T(8,128)S(1)}, f32[512,128]{1,0:T(8,128)S(1)}, u32[]{:S(2)}, u32[]{:S(2)}) collective-permute-start(f32[512,128]{1,0:T(8,128)S(1)} %collective-permute-done.8.refs_1_.refs_2_), channel_id=1, source_target_pairs={{0,7},{1,0},{2,1},{3,2},{4,3},{5,4},{6,5},{7,6},{8,15},{9,8},{10,9... | collective-permute-start | bytes 786440 | tf_op jit(solution)/shard_map/ppermute | solution.py:404
  47.7 2.8 %collective-permute-start.19 = (f32[48,128]{1,0:T(8,128)S(1)}, f32[48,128]{1,0:T(8,128)S(1)}, u32[]{:S(2)}, u32[]{:S(2)}) collective-permute-start(f32[48,128]{1,0:T(8,128)S(1)} %fusion.14), channel_id=1, source_target_pairs={{0,48},{8,56},{16,0},{24,8},{32,16},{40,24},{48,32},{56,40},{64,11... | collective-permute-start | bytes 73736 | tf_op jit(solution)/shard_map/ppermute | solution.py:279
  53.8 2.7 %collective-permute-start.16 = (f32[512,128]{1,0:T(8,128)S(1)}, f32[512,128]{1,0:T(8,128)S(1)}, u32[]{:S(2)}, u32[]{:S(2)}) collective-permute-start(f32[512,128]{1,0:T(8,128)S(1)} %collective-permute-done.10.refs_1_.refs_4_), channel_id=1, source_target_pairs={{0,7},{1,0},{2,1},{3,2},{4,3},{5,4},{6,5},{7,6},{8,15},{9,8},{10,9... | collective-permute-start | bytes 786440 | tf_op jit(solution)/shard_map/ppermute | solution.py:411
  56.6 6.7 %collective-permute-done.20 = f32[48,128]{1,0:T(8,128)S(1)} collective-permute-done((f32[48,128]{1,0:T(8,128)S(1)}, f32[48,128]{1,0:T(8,128)S(1)}, u32[]{:S(2)}, u32[]{:S(2)}) %collective-permute-start.20) | collective-permute-done | bytes 24608 | tf_op jit(solution)/shard_map/ppermute | solution.py:413
  64.6 2.5 %collective-permute-done.21 = f32[48,128]{1,0:T(8,128)S(1)} collective-permute-done((f32[48,128]{1,0:T(8,128)S(1)}, f32[48,128]{1,0:T(8,128)S(1)}, u32[]{:S(2)}, u32[]{:S(2)}) %collective-permute-start.21) | collective-permute-done | bytes 24608 | tf_op jit(solution)/shard_map/ppermute | solution.py:414
  73.7 6.6 %collective-permute-start.25 = (f32[16,40,128]{2,1,0:T(8,128)S(1)}, f32[16,40,128]{2,1,0:T(8,128)S(1)}, u32[]{:S(2)}, u32[]{:S(2)}) collective-permute-start(f32[16,40,128]{2,1,0:T(8,128)S(1)} %dynamic-slice_bitcast_fusion), channel_id=1, source_target_pairs={{0,8},{8,0},{16,24},{24,16},{32,40},{40,32},{48,56},{56,48},{64,72... | collective-permute-start | bytes 983048 | tf_op jit(solution)/shard_map/ppermute | solution.py:432
  84.0 3.1 %collective-permute-done.27 = f32[48,128]{1,0:T(8,128)S(1)} collective-permute-done((f32[48,128]{1,0:T(8,128)S(1)}, f32[48,128]{1,0:T(8,128)S(1)}, u32[]{:S(2)}, u32[]{:S(2)}) %collective-permute-start.27) | collective-permute-done | bytes 24608 | tf_op jit(solution)/shard_map/ppermute | solution.py:279
  89.8 5.1 %all-to-all-start = ((f32[16,40,128]{2,1,0:T(8,128)}), f32[16,40,128]{2,1,0:T(8,128)S(1)}, u32[]{:S(2)}, u32[]{:S(2)}) async-start(f32[16,40,128]{2,1,0:T(8,128)} %bitcast_add_fusion), calls=%async_computation | async-start | bytes 655360 | tf_op jit(solution)/shard_map/all_to_all | solution.py:283
  95.0 4.2 %factor.4.refs_0_ = f32[256,256]{1,0:T(8,128)S(1)} custom-call(s32[3]{0:T(128)S(1)} %pad_add_fusion.where_ref, f32[4,48,128]{2,1,0:T(8,128)S(1)} %pad_maximum_fusion.1.refs_0_, f32[4,48,128]{2,1,0:T(8,128)S(1)} %collective-permute-done.29.refs_1_), custom_call_target="tpu_custom_call" | custom-call | flops 4294967296 | bytes 524288 | tf_op jit(solution)/shard_map/factor/pallas_call | solution.py:367
  99.2 3.9 %factor.5.refs_0_ = f32[256,256]{1,0:T(8,128)S(1)} custom-call(s32[3]{0:T(128)S(1)} %pad_add_fusion.where_ref, f32[256,256]{1,0:T(8,128)S(1)} %factor.4.refs_0_), custom_call_target="tpu_custom_call" | custom-call | flops 4294967296 | bytes 524288 | tf_op jit(solution)/shard_map/factor/pallas_call | solution.py:367
  104.2 6.4 %all-to-all-start.1 = ((f32[16,40,128]{2,1,0:T(8,128)}), f32[16,40,128]{2,1,0:T(8,128)S(1)}, u32[]{:S(2)}, u32[]{:S(2)}) async-start(f32[16,40,128]{2,1,0:T(8,128)} %broadcast_in_dim.3), calls=%async_computation.1 | async-start | bytes 655360 | tf_op jit(solution)/shard_map/all_to_all | solution.py:283
  110.6 3.8 %factor.6.refs_0_ = f32[256,256]{1,0:T(8,128)S(1)} custom-call(s32[3]{0:T(128)S(1)} %pad_add_fusion.where_ref, f32[256,256]{1,0:T(8,128)S(1)} %factor.5.refs_0_), custom_call_target="tpu_custom_call" | custom-call | flops 4294967296 | bytes 524288 | tf_op jit(solution)/shard_map/factor/pallas_call | solution.py:367
  114.4 3.4 %factor.7.refs_12_ = f32[256,256]{1,0:T(8,128)S(1)} custom-call(s32[3]{0:T(128)S(1)} %pad_add_fusion.where_ref, f32[256,256]{1,0:T(8,128)S(1)} %factor.6.refs_0_), custom_call_target="tpu_custom_call" | custom-call | flops 4294967296 | bytes 524288 | tf_op jit(solution)/shard_map/factor/pallas_call | solution.py:367
  122.0 8.7 %residual.1 = (f32[1280,128]{1,0:T(8,128)}, f32[10240,128]{1,0:T(8,128)}) custom-call(s32[3]{0:T(128)S(1)} %pad_add_fusion.where_ref, f32[512,128]{1,0:T(8,128)S(1)} %pad_maximum_fusion.refs_0_.piece_ref, f32[512,128]{1,0:T(8,128)S(1)} %collective-permute-done.7.refs_0_.refs_1_, f32[512,128]{1,0:T(8,128)S(1)} %collective-permute-done.8.refs_1_.refs_2_, ...), custom_call_target="tpu_custom_call" | custom-call | flops 2013265920 | bytes 12582912 | tf_op jit(solution)/shard_map/residual/pallas_call | solution.py:444
  (75 shorter events, 36.4 us)
Async XLA Ops:
  2.1 13.6 %collective-permute-start.6 = (f32[256,128]{1,0:T(8,128)S(1)}, f32[256,128]{1,0:T(8,128)S(1)}, u32[]{:S(2)}, u32[]{:S(2)}) collective-permute-start(f32[256,128]{1,0:T(8,128)S(1)} %get-tuple-element.108), channel_id=1, source_target_pairs={{0,1},{1,2},{8,9},{9,10},{16,17},{17,18},{24,25},{25,26},{32,33},{... | collective-permute-start | bytes 393224 | tf_op jit(solution)/shard_map/ppermute | solution.py:295
  6.5 10.5 %collective-permute-start.5 = (f32[256,128]{1,0:T(8,128)S(1)}, f32[256,128]{1,0:T(8,128)S(1)}, u32[]{:S(2)}, u32[]{:S(2)}) collective-permute-start(f32[256,128]{1,0:T(8,128)S(1)} %get-tuple-element.109), channel_id=1, source_target_pairs={{0,2},{1,3},{8,10},{9,11},{16,18},{17,19},{24,26},{25,27},{32,34},... | collective-permute-start | bytes 393224 | tf_op jit(solution)/shard_map/ppermute | solution.py:295
  9.2 15.3 %collective-permute-start.4 = (f32[256,128]{1,0:T(8,128)S(1)}, f32[256,128]{1,0:T(8,128)S(1)}, u32[]{:S(2)}, u32[]{:S(2)}) collective-permute-start(f32[256,128]{1,0:T(8,128)S(1)} %get-tuple-element.110), channel_id=1, source_target_pairs={{0,3},{1,4},{8,11},{9,12},{16,19},{17,20},{24,27},{25,28},{32,35},... | collective-permute-start | bytes 393224 | tf_op jit(solution)/shard_map/ppermute | solution.py:295
  11.2 13.3 %collective-permute-start.3 = (f32[256,128]{1,0:T(8,128)S(1)}, f32[256,128]{1,0:T(8,128)S(1)}, u32[]{:S(2)}, u32[]{:S(2)}) collective-permute-start(f32[256,128]{1,0:T(8,128)S(1)} %get-tuple-element.111), channel_id=1, source_target_pairs={{0,4},{1,5},{8,12},{9,13},{16,20},{17,21},{24,28},{25,29},{32,36},... | collective-permute-start | bytes 393224 | tf_op jit(solution)/shard_map/ppermute | solution.py:295
  14.4 11.5 %collective-permute-start.2 = (f32[256,128]{1,0:T(8,128)S(1)}, f32[256,128]{1,0:T(8,128)S(1)}, u32[]{:S(2)}, u32[]{:S(2)}) collective-permute-start(f32[256,128]{1,0:T(8,128)S(1)} %get-tuple-element.112), channel_id=1, source_target_pairs={{0,5},{1,6},{8,13},{9,14},{16,21},{17,22},{24,29},{25,30},{32,37},... | collective-permute-start | bytes 393224 | tf_op jit(solution)/shard_map/ppermute | solution.py:295
  15.8 13.1 %collective-permute-start.1 = (f32[256,128]{1,0:T(8,128)S(1)}, f32[256,128]{1,0:T(8,128)S(1)}, u32[]{:S(2)}, u32[]{:S(2)}) collective-permute-start(f32[256,128]{1,0:T(8,128)S(1)} %get-tuple-element.113), channel_id=1, source_target_pairs={{0,6},{1,7},{8,14},{9,15},{16,22},{17,23},{24,30},{25,31},{32,38},... | collective-permute-start | bytes 393224 | tf_op jit(solution)/shard_map/ppermute | solution.py:295
  17.1 14.6 %collective-permute-start = (f32[256,128]{1,0:T(8,128)S(1)}, f32[256,128]{1,0:T(8,128)S(1)}, u32[]{:S(2)}, u32[]{:S(2)}) collective-permute-start(f32[256,128]{1,0:T(8,128)S(1)} %get-tuple-element.114), channel_id=1, source_target_pairs={{0,7},{1,0},{8,15},{9,8},{16,23},{17,16},{24,31},{25,24},{32,39},{... | collective-permute-start | bytes 393224 | tf_op jit(solution)/shard_map/ppermute | solution.py:295
  32.8 9.1 %collective-permute-start.8 = (f32[512,128]{1,0:T(8,128)S(1)}, f32[512,128]{1,0:T(8,128)S(1)}, u32[]{:S(2)}, u32[]{:S(2)}) collective-permute-start(f32[512,128]{1,0:T(8,128)S(1)} %pad_maximum_fusion.refs_0_.piece_ref), channel_id=1, source_target_pairs={{0,7},{1,0},{2,1},{3,2},{4,3},{5,4},{6,5},{7,6},{8,15},{9,8},{10,9... | collective-permute-start | bytes 786440 | tf_op jit(solution)/shard_map/ppermute | solution.py:395
  36.2 8.7 %collective-permute-start.7 = (f32[512,128]{1,0:T(8,128)S(1)}, f32[512,128]{1,0:T(8,128)S(1)}, u32[]{:S(2)}, u32[]{:S(2)}) collective-permute-start(f32[512,128]{1,0:T(8,128)S(1)} %pad_maximum_fusion.refs_0_.piece_ref), channel_id=1, source_target_pairs={{0,1},{1,2},{2,3},{3,4},{4,5},{5,6},{6,7},{7,0},{8,9},{9,10},{10,1... | collective-permute-start | bytes 786440 | tf_op jit(solution)/shard_map/ppermute | solution.py:395
  36.3 11.4 %collective-permute-start.14 = (f32[48,128]{1,0:T(8,128)S(1)}, f32[48,128]{1,0:T(8,128)S(1)}, u32[]{:S(2)}, u32[]{:S(2)}) collective-permute-start(f32[48,128]{1,0:T(8,128)S(1)} %get-tuple-element.115), channel_id=1, source_target_pairs={{0,192},{8,200},{16,208},{24,216},{32,224},{40,232},{48,240},{56,2... | collective-permute-start | bytes 73736 | tf_op jit(solution)/shard_map/ppermute | solution.py:399
  38.8 8.8 %collective-permute-start.13 = (f32[48,128]{1,0:T(8,128)S(1)}, f32[48,128]{1,0:T(8,128)S(1)}, u32[]{:S(2)}, u32[]{:S(2)}) collective-permute-start(f32[48,128]{1,0:T(8,128)S(1)} %get-tuple-element.116), channel_id=1, source_target_pairs={{0,64},{8,72},{16,80},{24,88},{32,96},{40,104},{48,112},{56,120},{... | collective-permute-start | bytes 73736 | tf_op jit(solution)/shard_map/ppermute | solution.py:399
  38.8 8.8 %collective-permute-start.12 = (f32[48,128]{1,0:T(8,128)S(1)}, f32[48,128]{1,0:T(8,128)S(1)}, u32[]{:S(2)}, u32[]{:S(2)}) collective-permute-start(f32[48,128]{1,0:T(8,128)S(1)} %get-tuple-element.117), channel_id=1, source_target_pairs={{0,128},{8,136},{16,144},{24,152},{32,160},{40,168},{48,176},{56,1... | collective-permute-start | bytes 73736 | tf_op jit(solution)/shard_map/ppermute | solution.py:399
  45.0 8.5 %collective-permute-start.9 = (f32[512,128]{1,0:T(8,128)S(1)}, f32[512,128]{1,0:T(8,128)S(1)}, u32[]{:S(2)}, u32[]{:S(2)}) collective-permute-start(f32[512,128]{1,0:T(8,128)S(1)} %collective-permute-done.7.refs_0_.refs_1_), channel_id=1, source_target_pairs={{0,1},{1,2},{2,3},{3,4},{4,5},{5,6},{6,7},{7,0},{8,9},{9,10},{10,1... | collective-permute-start | bytes 786440 | tf_op jit(solution)/shard_map/ppermute | solution.py:404
  45.0 8.5 %collective-permute-start.10 = (f32[512,128]{1,0:T(8,128)S(1)}, f32[512,128]{1,0:T(8,128)S(1)}, u32[]{:S(2)}, u32[]{:S(2)}) collective-permute-start(f32[512,128]{1,0:T(8,128)S(1)} %collective-permute-done.8.refs_1_.refs_2_), channel_id=1, source_target_pairs={{0,7},{1,0},{2,1},{3,2},{4,3},{5,4},{6,5},{7,6},{8,15},{9,8},{10,9... | collective-permute-start | bytes 786440 | tf_op jit(solution)/shard_map/ppermute | solution.py:404
  47.7 8.8 %collective-permute-start.19 = (f32[48,128]{1,0:T(8,128)S(1)}, f32[48,128]{1,0:T(8,128)S(1)}, u32[]{:S(2)}, u32[]{:S(2)}) collective-permute-start(f32[48,128]{1,0:T(8,128)S(1)} %fusion.14), channel_id=1, source_target_pairs={{0,48},{8,56},{16,0},{24,8},{32,16},{40,24},{48,32},{56,40},{64,11... | collective-permute-start | bytes 73736 | tf_op jit(solution)/shard_map/ppermute | solution.py:279
  50.5 6.0 %collective-permute-start.18 = (f32[48,128]{1,0:T(8,128)S(1)}, f32[48,128]{1,0:T(8,128)S(1)}, u32[]{:S(2)}, u32[]{:S(2)}) collective-permute-start(f32[48,128]{1,0:T(8,128)S(1)} %fusion.14), channel_id=1, source_target_pairs={{0,16},{8,24},{16,32},{24,40},{32,48},{40,56},{48,0},{56,8},{64,80... | collective-permute-start | bytes 73736 | tf_op jit(solution)/shard_map/ppermute | solution.py:279
  50.5 6.0 %collective-permute-start.17 = (f32[48,128]{1,0:T(8,128)S(1)}, f32[48,128]{1,0:T(8,128)S(1)}, u32[]{:S(2)}, u32[]{:S(2)}) collective-permute-start(f32[48,128]{1,0:T(8,128)S(1)} %fusion.14), channel_id=1, source_target_pairs={{0,32},{8,40},{16,48},{24,56},{32,0},{40,8},{48,16},{56,24},{64,96... | collective-permute-start | bytes 73736 | tf_op jit(solution)/shard_map/ppermute | solution.py:279
  53.5 13.6 %collective-permute-start.15 = (f32[512,128]{1,0:T(8,128)S(1)}, f32[512,128]{1,0:T(8,128)S(1)}, u32[]{:S(2)}, u32[]{:S(2)}) collective-permute-start(f32[512,128]{1,0:T(8,128)S(1)} %collective-permute-done.9.refs_0_.refs_3_), channel_id=1, source_target_pairs={{0,1},{1,2},{2,3},{3,4},{4,5},{5,6},{6,7},{7,0},{8,9},{9,10},{10,1... | collective-permute-start | bytes 786440 | tf_op jit(solution)/shard_map/ppermute | solution.py:411
  53.8 13.4 %collective-permute-start.16 = (f32[512,128]{1,0:T(8,128)S(1)}, f32[512,128]{1,0:T(8,128)S(1)}, u32[]{:S(2)}, u32[]{:S(2)}) collective-permute-start(f32[512,128]{1,0:T(8,128)S(1)} %collective-permute-done.10.refs_1_.refs_4_), channel_id=1, source_target_pairs={{0,7},{1,0},{2,1},{3,2},{4,3},{5,4},{6,5},{7,6},{8,15},{9,8},{10,9... | collective-permute-start | bytes 786440 | tf_op jit(solution)/shard_map/ppermute | solution.py:411
  56.5 6.8 %collective-permute-start.20 = (f32[48,128]{1,0:T(8,128)S(1)}, f32[48,128]{1,0:T(8,128)S(1)}, u32[]{:S(2)}, u32[]{:S(2)}) collective-permute-start(f32[48,128]{1,0:T(8,128)S(1)} %add_add_fusion), channel_id=1, source_target_pairs={{0,4},{1,5},{2,6},{3,7},{4,0},{5,1},{6,2},{7,3},{8,12},{9,13},{10,... | collective-permute-start | bytes 73736 | tf_op jit(solution)/shard_map/ppermute | solution.py:413
  73.7 13.6 %collective-permute-start.25 = (f32[16,40,128]{2,1,0:T(8,128)S(1)}, f32[16,40,128]{2,1,0:T(8,128)S(1)}, u32[]{:S(2)}, u32[]{:S(2)}) collective-permute-start(f32[16,40,128]{2,1,0:T(8,128)S(1)} %dynamic-slice_bitcast_fusion), channel_id=1, source_target_pairs={{0,8},{8,0},{16,24},{24,16},{32,40},{40,32},{48,56},{56,48},{64,72... | collective-permute-start | bytes 983048 | tf_op jit(solution)/shard_map/ppermute | solution.py:432
  88.1 6.9 %collective-permute-start.29 = (f32[4,48,128]{2,1,0:T(8,128)S(1)}, f32[4,48,128]{2,1,0:T(8,128)S(1)}, u32[]{:S(2)}, u32[]{:S(2)}) collective-permute-start(f32[4,48,128]{2,1,0:T(8,128)S(1)} %pad_maximum_fusion.1.refs_0_), channel_id=1, source_target_pairs={{0,8},{8,0},{16,24},{24,16},{32,40},{40,32},{48,56},{56,48},{64,72... | collective-permute-start | bytes 294920 | tf_op jit(solution)/shard_map/ppermute | solution.py:435
  89.8 13.6 %all-to-all-start = ((f32[16,40,128]{2,1,0:T(8,128)}), f32[16,40,128]{2,1,0:T(8,128)S(1)}, u32[]{:S(2)}, u32[]{:S(2)}) async-start(f32[16,40,128]{2,1,0:T(8,128)} %bitcast_add_fusion), calls=%async_computation | async-start | bytes 655360 | tf_op jit(solution)/shard_map/all_to_all | solution.py:283
  104.2 14.2 %all-to-all-start.1 = ((f32[16,40,128]{2,1,0:T(8,128)}), f32[16,40,128]{2,1,0:T(8,128)S(1)}, u32[]{:S(2)}, u32[]{:S(2)}) async-start(f32[16,40,128]{2,1,0:T(8,128)} %broadcast_in_dim.3), calls=%async_computation.1 | async-start | bytes 655360 | tf_op jit(solution)/shard_map/all_to_all | solution.py:283
  (9 other events, 35.7 us)

commit v2 on v0

--- a/solution.py
+++ b/solution.py
@@ -9,8 +9,8 @@
 from jax.sharding import PartitionSpec as P
 
 LANES = 128
-STEP = 32
-GROUP = 4
+STEP = 64
+GROUP = 8
 SPAN = 64
 HIGHEST = lax.Precision.HIGHEST
 
@@ -77,12 +77,16 @@
     copies = [fetch(matrix_ref, window.at[i], sems.at[i], i, long) for i in range(chunks)]
     for copy in copies:
         copy.start()
-    for i, copy in enumerate(copies):
-        copy.wait()
+
+    def step(i, carry):
+        fetch(matrix_ref, window.at[i], sems.at[i], i, long).wait()
         for b in range(blocks):
             high, low = split(window[i, pl.ds(b, rows, stride=blocks), :])
             high_ref[i, :, LANES * b : LANES * (b + 1)] = high
             low_ref[i, :, LANES * b : LANES * (b + 1)] = low
+        return carry
+
+    lax.fori_loop(0, chunks, step, 0)
 
 
 def collect_kernel(hop, n_col, shapes, where_ref, *refs):
@@ -428,18 +432,16 @@
     took = [
         lax.ppermute(pick(part, steps[s + 1]), "row", p) for s, p in enumerate(along_x)
     ]
-    mine = mine + got
+    mine = mine + after(got, part)
     other = lax.ppermute(mine, "row", swap)
-    work = factor(0, mine, other)
-    part = after(total(pick(part, steps[0]), took), work)
+    part = total(pick(part, steps[0]), took)
     took = send(part, along_y)
-    work = factor(SPAN, work)
+    work = factor(SPAN, factor(0, mine, after(other, part)))
     part = after(total(part, took), work)
     took = send(part, along_x)
-    work = factor(2 * SPAN, work)
+    work = factor(3 * SPAN, factor(2 * SPAN, after(work, part)))
     cross_mine = after(jnp.stack([part, *took]), work)
     cross_other = lax.ppermute(cross_mine, "row", swap)
-    work = factor(3 * SPAN, work)
     shapes = [len(p) for p in every]
     scaled, residual = pl.pallas_call(
         functools.partial(

time: 125 us -> 120 us (0.960)
  Pallas kernels: 33.3 us -> 28.8 us
    pallas_call x4, Pallas kernels: 15.4 us -> 10.9 us  [factor(): pl.pallas_call(functools.partial(factor_kernel, begin, begin + SPAN), out...]
    ppermute x1, waiting for transfers between devices: 4.4 us -> 0.01 us  [per_device(): got = lax.ppermute(mine, 'col', flips[2])]
    ppermute x3, waiting for transfers between devices: 1.01 us -> 2.92 us  [per_device(): lax.ppermute(pick(part, steps[s + 1]), 'row', p)]
    ppermute x1, waiting for transfers between devices: 0.01 us -> 1.26 us  [per_device(): cross_other = lax.ppermute(cross_mine, 'row', swap)]
  transfers between devices with their start and end apart: 37 -> 37, of which waited for: 12 -> 12; matrix products, arithmetic and copies ran while one was open for 2% -> 3% of each run, Pallas kernels for 19% -> 16%
where the time goes in v2:
time: 120 us; the launch traced here: 119 us
  starting transfers between devices  61.1 us (51%)
  Pallas kernels  28.8 us (24%)
  waiting for transfers between devices  23.7 us (20%)
  local copies, waits for them, and re-layouts  4.25 us (4%)
  between operations  1.28 us (1%)
    ppermute x7, starting transfers between devices, hand_out(): got = lax.ppermute(pick(pieces, spots[s]), 'col', pairs)  16.8 us
    ppermute x12, starting transfers between devices, send(): return [lax.ppermute(value, 'row', perm) for perm in perms]  14.7 us
    pallas_call x4, Pallas kernels, factor(): pl.pallas_call(functools.partial(factor_kernel, begin, begin + SPAN), out...  10.9 us
    pallas_call x1, Pallas kernels, per_device(): pl.pallas_call(functools.partial(residual_kernel, n_col, blocks, 1.0 / ma...  8.67 us
    ppermute x7, waiting for transfers between devices, hand_out(): got = lax.ppermute(pick(pieces, spots[s]), 'col', pairs)  7.18 us
    ppermute x1, starting transfers between devices, per_device(): part = pick(whole, this) + lax.ppermute(pick(whole, that), 'row', swap)  6.75 us
    pallas_call x5, Pallas kernels, collect(): pl.pallas_call(functools.partial(collect_kernel, hop, n_col, shapes), out...  6.18 us
    ppermute x2, starting transfers between devices, per_device(): lax.ppermute(right, 'col', down)  5.34 us
  transfers between devices with their start and end apart: 37, of which 12 were waited for; matrix products, arithmetic and copies ran while one was open for 3% of the time, Pallas kernels for 16%

profile of v2, /device:TPU:1, one launch (start us, length us, event | category | flops | bytes accessed | tf_op | source)
XLA Modules:
  0.0 119.4 jit_solution(14396760245427444801)
XLA Ops:
  2.1 4.4 %collective-permute-start.6 = (f32[256,128]{1,0:T(8,128)S(1)}, f32[256,128]{1,0:T(8,128)S(1)}, u32[]{:S(2)}, u32[]{:S(2)}) collective-permute-start(f32[256,128]{1,0:T(8,128)S(1)} %get-tuple-element.110), channel_id=1, source_target_pairs={{0,1},{1,2},{8,9},{9,10},{16,17},{17,18},{24,25},{25,26},{32,33},{... | collective-permute-start | bytes 393224 | tf_op jit(solution)/shard_map/ppermute | solution.py:295
  6.5 2.6 %collective-permute-start.5 = (f32[256,128]{1,0:T(8,128)S(1)}, f32[256,128]{1,0:T(8,128)S(1)}, u32[]{:S(2)}, u32[]{:S(2)}) collective-permute-start(f32[256,128]{1,0:T(8,128)S(1)} %get-tuple-element.111), channel_id=1, source_target_pairs={{0,2},{1,3},{8,10},{9,11},{16,18},{17,19},{24,26},{25,27},{32,34},... | collective-permute-start | bytes 393224 | tf_op jit(solution)/shard_map/ppermute | solution.py:295
  11.2 3.2 %collective-permute-start.3 = (f32[256,128]{1,0:T(8,128)S(1)}, f32[256,128]{1,0:T(8,128)S(1)}, u32[]{:S(2)}, u32[]{:S(2)}) collective-permute-start(f32[256,128]{1,0:T(8,128)S(1)} %get-tuple-element.113), channel_id=1, source_target_pairs={{0,4},{1,5},{8,12},{9,13},{16,20},{17,21},{24,28},{25,29},{32,36},... | collective-permute-start | bytes 393224 | tf_op jit(solution)/shard_map/ppermute | solution.py:295
  19.0 2.8 %copy.7 = f32[2048,5,1,128]{3,0,2,1:T(8,128)S(1)} copy(f32[2048,5,1,128]{3,2,1,0:T(1,128)} %param.1) | data formatting | bytes 10485760 | tf_op jit(solution)/shard_map/optimization_barrier | solution.py:323
  21.8 2.7 %stage.1 = (bf16[8,256,640]{2,1,0:T(8,128)(2,1)S(1)}, bf16[8,256,640]{2,1,0:T(8,128)(2,1)S(1)}) custom-call(f32[10240,128]{1,0:T(8,128)} %bitcast.81), custom_call_target="tpu_custom_call" | custom-call | flops 10485760 | bytes 10485760 | tf_op jit(solution)/shard_map/stage/pallas_call | solution.py:336
  25.9 3.0 %collective-permute-done.1 = f32[256,128]{1,0:T(8,128)S(1)} collective-permute-done((f32[256,128]{1,0:T(8,128)S(1)}, f32[256,128]{1,0:T(8,128)S(1)}, u32[]{:S(2)}, u32[]{:S(2)}) %collective-permute-start.1) | collective-permute-done | bytes 131104 | tf_op jit(solution)/shard_map/ppermute | solution.py:295
  28.9 2.8 %collective-permute-done = f32[256,128]{1,0:T(8,128)S(1)} collective-permute-done((f32[256,128]{1,0:T(8,128)S(1)}, f32[256,128]{1,0:T(8,128)S(1)}, u32[]{:S(2)}, u32[]{:S(2)}) %collective-permute-start) | collective-permute-done | bytes 131104 | tf_op jit(solution)/shard_map/ppermute | solution.py:295
  32.8 3.4 %collective-permute-start.8 = (f32[512,128]{1,0:T(8,128)S(1)}, f32[512,128]{1,0:T(8,128)S(1)}, u32[]{:S(2)}, u32[]{:S(2)}) collective-permute-start(f32[512,128]{1,0:T(8,128)S(1)} %pad_maximum_fusion.1.refs_0_.piece_ref), channel_id=1, source_target_pairs={{0,7},{1,0},{2,1},{3,2},{4,3},{5,4},{6,5},{7,6},{8,15},{9,8},{10,9... | collective-permute-start | bytes 786440 | tf_op jit(solution)/shard_map/ppermute | solution.py:395
  36.2 2.6 %collective-permute-start.14 = (f32[192,128]{1,0:T(8,128)S(1)}, f32[192,128]{1,0:T(8,128)S(1)}, u32[]{:S(2)}, u32[]{:S(2)}) collective-permute-start(f32[192,128]{1,0:T(8,128)S(1)} %bitcast_add_fusion.1), channel_id=1, source_target_pairs={{0,192},{8,200},{16,208},{24,216},{32,224},{40,232},{48,240},{56,2... | collective-permute-start | bytes 294920 | tf_op jit(solution)/shard_map/ppermute | solution.py:283
  41.9 3.1 %collective-permute-done.7.refs_0_.refs_1_ = f32[512,128]{1,0:T(8,128)S(1)} collective-permute-done((f32[512,128]{1,0:T(8,128)S(1)}, f32[512,128]{1,0:T(8,128)S(1)}, u32[]{:S(2)}, u32[]{:S(2)}) %collective-permute-start.7) | collective-permute-done | bytes 262176 | tf_op jit(solution)/shard_map/ppermute | solution.py:395
  45.0 2.7 %collective-permute-start.10 = (f32[512,128]{1,0:T(8,128)S(1)}, f32[512,128]{1,0:T(8,128)S(1)}, u32[]{:S(2)}, u32[]{:S(2)}) collective-permute-start(f32[512,128]{1,0:T(8,128)S(1)} %collective-permute-done.8.refs_1_.refs_2_), channel_id=1, source_target_pairs={{0,7},{1,0},{2,1},{3,2},{4,3},{5,4},{6,5},{7,6},{8,15},{9,8},{10,9... | collective-permute-start | bytes 786440 | tf_op jit(solution)/shard_map/ppermute | solution.py:403
  47.7 2.8 %collective-permute-start.19 = (f32[192,128]{1,0:T(8,128)S(1)}, f32[192,128]{1,0:T(8,128)S(1)}, u32[]{:S(2)}, u32[]{:S(2)}) collective-permute-start(f32[192,128]{1,0:T(8,128)S(1)} %add_add_fusion.1), channel_id=1, source_target_pairs={{0,48},{8,56},{16,0},{24,8},{32,16},{40,24},{48,32},{56,40},{64,11... | collective-permute-start | bytes 294920 | tf_op jit(solution)/shard_map/ppermute | solution.py:283
  53.6 2.7 %collective-permute-start.16 = (f32[512,128]{1,0:T(8,128)S(1)}, f32[512,128]{1,0:T(8,128)S(1)}, u32[]{:S(2)}, u32[]{:S(2)}) collective-permute-start(f32[512,128]{1,0:T(8,128)S(1)} %collective-permute-done.10.refs_1_.refs_4_), channel_id=1, source_target_pairs={{0,7},{1,0},{2,1},{3,2},{4,3},{5,4},{6,5},{7,6},{8,15},{9,8},{10,9... | collective-permute-start | bytes 786440 | tf_op jit(solution)/shard_map/ppermute | solution.py:410
  62.0 3.6 %collective-permute-start.21 = (f32[256,128]{1,0:T(8,128)S(1)}, f32[256,128]{1,0:T(8,128)S(1)}, u32[]{:S(2)}, u32[]{:S(2)}) collective-permute-start(f32[256,128]{1,0:T(8,128)S(1)} %slice.23), channel_id=1, source_target_pairs={{0,7},{1,0},{2,1},{3,2},{4,3},{5,4},{6,5},{7,6},{8,15},{9,8},{10,9... | collective-permute-start | bytes 393224 | tf_op jit(solution)/shard_map/ppermute | solution.py:419
  67.2 3.5 %collective-permute-done.23 = f32[192,128]{1,0:T(8,128)S(1)} collective-permute-done((f32[192,128]{1,0:T(8,128)S(1)}, f32[192,128]{1,0:T(8,128)S(1)}, u32[]{:S(2)}, u32[]{:S(2)}) %collective-permute-start.23) | collective-permute-done | bytes 98336 | tf_op jit(solution)/shard_map/ppermute | solution.py:422
  71.8 6.7 %collective-permute-start.24 = (f32[4,160,128]{2,1,0:T(8,128)S(1)}, f32[4,160,128]{2,1,0:T(8,128)S(1)}, u32[]{:S(2)}, u32[]{:S(2)}) collective-permute-start(f32[4,160,128]{2,1,0:T(8,128)S(1)} %dynamic-slice_bitcast_fusion), channel_id=1, source_target_pairs={{0,8},{8,0},{16,24},{24,16},{32,40},{40,32},{48,56},{56,48},{64,72... | collective-permute-start | bytes 983048 | tf_op jit(solution)/shard_map/ppermute | solution.py:431
  79.9 2.6 %collective-permute-start.27 = (f32[160,128]{1,0:T(8,128)S(1)}, f32[160,128]{1,0:T(8,128)S(1)}, u32[]{:S(2)}, u32[]{:S(2)}) collective-permute-start(f32[160,128]{1,0:T(8,128)S(1)} %get-tuple-element.117), channel_id=1, source_target_pairs={{0,192},{8,200},{16,208},{24,216},{32,224},{40,232},{48,240},{56,2... | collective-permute-start | bytes 245768 | tf_op jit(solution)/shard_map/ppermute | solution.py:433
  85.5 2.6 %collective-permute-done.26 = f32[160,128]{1,0:T(8,128)S(1)} collective-permute-done((f32[160,128]{1,0:T(8,128)S(1)}, f32[160,128]{1,0:T(8,128)S(1)}, u32[]{:S(2)}, u32[]{:S(2)}) %collective-permute-start.26) | collective-permute-done | bytes 81952 | tf_op jit(solution)/shard_map/ppermute | solution.py:433
  92.2 2.9 %factor.4.refs_0_ = f32[256,256]{1,0:T(8,128)S(1)} custom-call(s32[3]{0:T(128)S(1)} %pad_add_fusion.where_ref, f32[192,128]{1,0:T(8,128)S(1)} %add.108.refs_0_, f32[192,128]{1,0:T(8,128)S(1)} %collective-permute-done.32.refs_1_), custom_call_target="tpu_custom_call" | custom-call | flops 4294967296 | bytes 524288 | tf_op jit(solution)/shard_map/factor/pallas_call | solution.py:367
  95.1 2.8 %factor.5.refs_0_ = f32[256,256]{1,0:T(8,128)S(1)} custom-call(s32[3]{0:T(128)S(1)} %pad_add_fusion.where_ref, f32[256,256]{1,0:T(8,128)S(1)} %factor.4.refs_0_), custom_call_target="tpu_custom_call" | custom-call | flops 4294967296 | bytes 524288 | tf_op jit(solution)/shard_map/factor/pallas_call | solution.py:367
  100.2 2.8 %factor.6.refs_0_ = f32[256,256]{1,0:T(8,128)S(1)} custom-call(s32[3]{0:T(128)S(1)} %pad_add_fusion.where_ref, f32[256,256]{1,0:T(8,128)S(1)} %factor.5.refs_0_), custom_call_target="tpu_custom_call" | custom-call | flops 4294967296 | bytes 524288 | tf_op jit(solution)/shard_map/factor/pallas_call | solution.py:367
  102.9 2.5 %factor.7.refs_12_ = f32[256,256]{1,0:T(8,128)S(1)} custom-call(s32[3]{0:T(128)S(1)} %pad_add_fusion.where_ref, f32[256,256]{1,0:T(8,128)S(1)} %factor.6.refs_0_), custom_call_target="tpu_custom_call" | custom-call | flops 4294967296 | bytes 524288 | tf_op jit(solution)/shard_map/factor/pallas_call | solution.py:367
  105.5 3.9 %collective-permute-start.36 = (f32[4,160,128]{2,1,0:T(8,128)S(1)}, f32[4,160,128]{2,1,0:T(8,128)S(1)}, u32[]{:S(2)}, u32[]{:S(2)}) collective-permute-start(f32[4,160,128]{2,1,0:T(8,128)S(1)} %pad_maximum_fusion.refs_10_), channel_id=1, source_target_pairs={{0,8},{8,0},{16,24},{24,16},{32,40},{40,32},{48,56},{56,48},{64,72... | collective-permute-start | bytes 983048 | tf_op jit(solution)/shard_map/ppermute | solution.py:444
  110.6 8.7 %residual.1 = (f32[1280,128]{1,0:T(8,128)}, f32[10240,128]{1,0:T(8,128)}) custom-call(s32[3]{0:T(128)S(1)} %pad_add_fusion.where_ref, f32[512,128]{1,0:T(8,128)S(1)} %pad_maximum_fusion.1.refs_0_.piece_ref, f32[512,128]{1,0:T(8,128)S(1)} %collective-permute-done.7.refs_0_.refs_1_, f32[512,128]{1,0:T(8,128)S(1)} %collective-permute-done.8.refs_1_.refs_2_, ...), custom_call_target="tpu_custom_call" | custom-call | flops 2013265920 | bytes 12582912 | tf_op jit(solution)/shard_map/residual/pallas_call | solution.py:446
  (83 shorter events, 36.9 us)
Async XLA Ops:
  2.1 13.6 %collective-permute-start.6 = (f32[256,128]{1,0:T(8,128)S(1)}, f32[256,128]{1,0:T(8,128)S(1)}, u32[]{:S(2)}, u32[]{:S(2)}) collective-permute-start(f32[256,128]{1,0:T(8,128)S(1)} %get-tuple-element.110), channel_id=1, source_target_pairs={{0,1},{1,2},{8,9},{9,10},{16,17},{17,18},{24,25},{25,26},{32,33},{... | collective-permute-start | bytes 393224 | tf_op jit(solution)/shard_map/ppermute | solution.py:295
  6.5 10.5 %collective-permute-start.5 = (f32[256,128]{1,0:T(8,128)S(1)}, f32[256,128]{1,0:T(8,128)S(1)}, u32[]{:S(2)}, u32[]{:S(2)}) collective-permute-start(f32[256,128]{1,0:T(8,128)S(1)} %get-tuple-element.111), channel_id=1, source_target_pairs={{0,2},{1,3},{8,10},{9,11},{16,18},{17,19},{24,26},{25,27},{32,34},... | collective-permute-start | bytes 393224 | tf_op jit(solution)/shard_map/ppermute | solution.py:295
  9.2 15.3 %collective-permute-start.4 = (f32[256,128]{1,0:T(8,128)S(1)}, f32[256,128]{1,0:T(8,128)S(1)}, u32[]{:S(2)}, u32[]{:S(2)}) collective-permute-start(f32[256,128]{1,0:T(8,128)S(1)} %get-tuple-element.112), channel_id=1, source_target_pairs={{0,3},{1,4},{8,11},{9,12},{16,19},{17,20},{24,27},{25,28},{32,35},... | collective-permute-start | bytes 393224 | tf_op jit(solution)/shard_map/ppermute | solution.py:295
  11.2 13.3 %collective-permute-start.3 = (f32[256,128]{1,0:T(8,128)S(1)}, f32[256,128]{1,0:T(8,128)S(1)}, u32[]{:S(2)}, u32[]{:S(2)}) collective-permute-start(f32[256,128]{1,0:T(8,128)S(1)} %get-tuple-element.113), channel_id=1, source_target_pairs={{0,4},{1,5},{8,12},{9,13},{16,20},{17,21},{24,28},{25,29},{32,36},... | collective-permute-start | bytes 393224 | tf_op jit(solution)/shard_map/ppermute | solution.py:295
  14.4 11.5 %collective-permute-start.2 = (f32[256,128]{1,0:T(8,128)S(1)}, f32[256,128]{1,0:T(8,128)S(1)}, u32[]{:S(2)}, u32[]{:S(2)}) collective-permute-start(f32[256,128]{1,0:T(8,128)S(1)} %get-tuple-element.114), channel_id=1, source_target_pairs={{0,5},{1,6},{8,13},{9,14},{16,21},{17,22},{24,29},{25,30},{32,37},... | collective-permute-start | bytes 393224 | tf_op jit(solution)/shard_map/ppermute | solution.py:295
  15.8 13.1 %collective-permute-start.1 = (f32[256,128]{1,0:T(8,128)S(1)}, f32[256,128]{1,0:T(8,128)S(1)}, u32[]{:S(2)}, u32[]{:S(2)}) collective-permute-start(f32[256,128]{1,0:T(8,128)S(1)} %get-tuple-element.115), channel_id=1, source_target_pairs={{0,6},{1,7},{8,14},{9,15},{16,22},{17,23},{24,30},{25,31},{32,38},... | collective-permute-start | bytes 393224 | tf_op jit(solution)/shard_map/ppermute | solution.py:295
  17.1 14.6 %collective-permute-start = (f32[256,128]{1,0:T(8,128)S(1)}, f32[256,128]{1,0:T(8,128)S(1)}, u32[]{:S(2)}, u32[]{:S(2)}) collective-permute-start(f32[256,128]{1,0:T(8,128)S(1)} %get-tuple-element.116), channel_id=1, source_target_pairs={{0,7},{1,0},{8,15},{9,8},{16,23},{17,16},{24,31},{25,24},{32,39},{... | collective-permute-start | bytes 393224 | tf_op jit(solution)/shard_map/ppermute | solution.py:295
  32.8 9.1 %collective-permute-start.8 = (f32[512,128]{1,0:T(8,128)S(1)}, f32[512,128]{1,0:T(8,128)S(1)}, u32[]{:S(2)}, u32[]{:S(2)}) collective-permute-start(f32[512,128]{1,0:T(8,128)S(1)} %pad_maximum_fusion.1.refs_0_.piece_ref), channel_id=1, source_target_pairs={{0,7},{1,0},{2,1},{3,2},{4,3},{5,4},{6,5},{7,6},{8,15},{9,8},{10,9... | collective-permute-start | bytes 786440 | tf_op jit(solution)/shard_map/ppermute | solution.py:395
  36.2 8.7 %collective-permute-start.7 = (f32[512,128]{1,0:T(8,128)S(1)}, f32[512,128]{1,0:T(8,128)S(1)}, u32[]{:S(2)}, u32[]{:S(2)}) collective-permute-start(f32[512,128]{1,0:T(8,128)S(1)} %pad_maximum_fusion.1.refs_0_.piece_ref), channel_id=1, source_target_pairs={{0,1},{1,2},{2,3},{3,4},{4,5},{5,6},{6,7},{7,0},{8,9},{9,10},{10,1... | collective-permute-start | bytes 786440 | tf_op jit(solution)/shard_map/ppermute | solution.py:395
  36.2 11.4 %collective-permute-start.14 = (f32[192,128]{1,0:T(8,128)S(1)}, f32[192,128]{1,0:T(8,128)S(1)}, u32[]{:S(2)}, u32[]{:S(2)}) collective-permute-start(f32[192,128]{1,0:T(8,128)S(1)} %bitcast_add_fusion.1), channel_id=1, source_target_pairs={{0,192},{8,200},{16,208},{24,216},{32,224},{40,232},{48,240},{56,2... | collective-permute-start | bytes 294920 | tf_op jit(solution)/shard_map/ppermute | solution.py:283
  38.8 8.8 %collective-permute-start.13 = (f32[192,128]{1,0:T(8,128)S(1)}, f32[192,128]{1,0:T(8,128)S(1)}, u32[]{:S(2)}, u32[]{:S(2)}) collective-permute-start(f32[192,128]{1,0:T(8,128)S(1)} %bitcast_add_fusion.1), channel_id=1, source_target_pairs={{0,64},{8,72},{16,80},{24,88},{32,96},{40,104},{48,112},{56,120},{... | collective-permute-start | bytes 294920 | tf_op jit(solution)/shard_map/ppermute | solution.py:283
  38.8 8.8 %collective-permute-start.12 = (f32[192,128]{1,0:T(8,128)S(1)}, f32[192,128]{1,0:T(8,128)S(1)}, u32[]{:S(2)}, u32[]{:S(2)}) collective-permute-start(f32[192,128]{1,0:T(8,128)S(1)} %bitcast_add_fusion.1), channel_id=1, source_target_pairs={{0,128},{8,136},{16,144},{24,152},{32,160},{40,168},{48,176},{56,1... | collective-permute-start | bytes 294920 | tf_op jit(solution)/shard_map/ppermute | solution.py:283
  45.0 8.5 %collective-permute-start.9 = (f32[512,128]{1,0:T(8,128)S(1)}, f32[512,128]{1,0:T(8,128)S(1)}, u32[]{:S(2)}, u32[]{:S(2)}) collective-permute-start(f32[512,128]{1,0:T(8,128)S(1)} %collective-permute-done.7.refs_0_.refs_1_), channel_id=1, source_target_pairs={{0,1},{1,2},{2,3},{3,4},{4,5},{5,6},{6,7},{7,0},{8,9},{9,10},{10,1... | collective-permute-start | bytes 786440 | tf_op jit(solution)/shard_map/ppermute | solution.py:403
  45.0 8.5 %collective-permute-start.10 = (f32[512,128]{1,0:T(8,128)S(1)}, f32[512,128]{1,0:T(8,128)S(1)}, u32[]{:S(2)}, u32[]{:S(2)}) collective-permute-start(f32[512,128]{1,0:T(8,128)S(1)} %collective-permute-done.8.refs_1_.refs_2_), channel_id=1, source_target_pairs={{0,7},{1,0},{2,1},{3,2},{4,3},{5,4},{6,5},{7,6},{8,15},{9,8},{10,9... | collective-permute-start | bytes 786440 | tf_op jit(solution)/shard_map/ppermute | solution.py:403
  47.7 8.6 %collective-permute-start.19 = (f32[192,128]{1,0:T(8,128)S(1)}, f32[192,128]{1,0:T(8,128)S(1)}, u32[]{:S(2)}, u32[]{:S(2)}) collective-permute-start(f32[192,128]{1,0:T(8,128)S(1)} %add_add_fusion.1), channel_id=1, source_target_pairs={{0,48},{8,56},{16,0},{24,8},{32,16},{40,24},{48,32},{56,40},{64,11... | collective-permute-start | bytes 294920 | tf_op jit(solution)/shard_map/ppermute | solution.py:283
  53.6 8.4 %collective-permute-start.16 = (f32[512,128]{1,0:T(8,128)S(1)}, f32[512,128]{1,0:T(8,128)S(1)}, u32[]{:S(2)}, u32[]{:S(2)}) collective-permute-start(f32[512,128]{1,0:T(8,128)S(1)} %collective-permute-done.10.refs_1_.refs_4_), channel_id=1, source_target_pairs={{0,7},{1,0},{2,1},{3,2},{4,3},{5,4},{6,5},{7,6},{8,15},{9,8},{10,9... | collective-permute-start | bytes 786440 | tf_op jit(solution)/shard_map/ppermute | solution.py:410
  56.3 9.4 %collective-permute-start.22 = (f32[192,128]{1,0:T(8,128)S(1)}, f32[192,128]{1,0:T(8,128)S(1)}, u32[]{:S(2)}, u32[]{:S(2)}) collective-permute-start(f32[192,128]{1,0:T(8,128)S(1)} %add_add_fusion), channel_id=1, source_target_pairs={{0,4},{1,5},{2,6},{3,7},{4,0},{5,1},{6,2},{7,3},{8,12},{9,13},{10,... | collective-permute-start | bytes 294920 | tf_op jit(solution)/shard_map/ppermute | solution.py:412
  62.0 8.7 %collective-permute-start.21 = (f32[256,128]{1,0:T(8,128)S(1)}, f32[256,128]{1,0:T(8,128)S(1)}, u32[]{:S(2)}, u32[]{:S(2)}) collective-permute-start(f32[256,128]{1,0:T(8,128)S(1)} %slice.23), channel_id=1, source_target_pairs={{0,7},{1,0},{2,1},{3,2},{4,3},{5,4},{6,5},{7,6},{8,15},{9,8},{10,9... | collective-permute-start | bytes 393224 | tf_op jit(solution)/shard_map/ppermute | solution.py:419
  71.8 8.0 %collective-permute-start.24 = (f32[4,160,128]{2,1,0:T(8,128)S(1)}, f32[4,160,128]{2,1,0:T(8,128)S(1)}, u32[]{:S(2)}, u32[]{:S(2)}) collective-permute-start(f32[4,160,128]{2,1,0:T(8,128)S(1)} %dynamic-slice_bitcast_fusion), channel_id=1, source_target_pairs={{0,8},{8,0},{16,24},{24,16},{32,40},{40,32},{48,56},{56,48},{64,72... | collective-permute-start | bytes 983048 | tf_op jit(solution)/shard_map/ppermute | solution.py:431
  84.2 8.0 %collective-permute-start.32 = (f32[192,128]{1,0:T(8,128)S(1)}, f32[192,128]{1,0:T(8,128)S(1)}, u32[]{:S(2)}, u32[]{:S(2)}) collective-permute-start(f32[192,128]{1,0:T(8,128)S(1)} %add.108.refs_0_), channel_id=1, source_target_pairs={{0,8},{8,0},{16,24},{24,16},{32,40},{40,32},{48,56},{56,48},{64,72... | collective-permute-start | bytes 294920 | tf_op jit(solution)/shard_map/ppermute | solution.py:436
  88.4 9.4 %collective-permute-start.30 = (f32[160,128]{1,0:T(8,128)S(1)}, f32[160,128]{1,0:T(8,128)S(1)}, u32[]{:S(2)}, u32[]{:S(2)}) collective-permute-start(f32[160,128]{1,0:T(8,128)S(1)} %fusion.14), channel_id=1, source_target_pairs={{0,48},{8,56},{16,0},{24,8},{32,16},{40,24},{48,32},{56,40},{64,11... | collective-permute-start | bytes 245768 | tf_op jit(solution)/shard_map/ppermute | solution.py:283
  90.5 7.3 %collective-permute-start.29 = (f32[160,128]{1,0:T(8,128)S(1)}, f32[160,128]{1,0:T(8,128)S(1)}, u32[]{:S(2)}, u32[]{:S(2)}) collective-permute-start(f32[160,128]{1,0:T(8,128)S(1)} %fusion.14), channel_id=1, source_target_pairs={{0,16},{8,24},{16,32},{24,40},{32,48},{40,56},{48,0},{56,8},{64,80... | collective-permute-start | bytes 245768 | tf_op jit(solution)/shard_map/ppermute | solution.py:283
  90.5 7.4 %collective-permute-start.28 = (f32[160,128]{1,0:T(8,128)S(1)}, f32[160,128]{1,0:T(8,128)S(1)}, u32[]{:S(2)}, u32[]{:S(2)}) collective-permute-start(f32[160,128]{1,0:T(8,128)S(1)} %fusion.14), channel_id=1, source_target_pairs={{0,32},{8,40},{16,48},{24,56},{32,0},{40,8},{48,16},{56,24},{64,96... | collective-permute-start | bytes 245768 | tf_op jit(solution)/shard_map/ppermute | solution.py:283
  97.9 7.5 %collective-permute-start.35 = (f32[160,128]{1,0:T(8,128)S(1)}, f32[160,128]{1,0:T(8,128)S(1)}, u32[]{:S(2)}, u32[]{:S(2)}) collective-permute-start(f32[160,128]{1,0:T(8,128)S(1)} %add_add_fusion.2), channel_id=1, source_target_pairs={{0,192},{8,200},{16,208},{24,216},{32,224},{40,232},{48,240},{56,2... | collective-permute-start | bytes 245768 | tf_op jit(solution)/shard_map/ppermute | solution.py:283
  (13 other events, 72.0 us)

commit v3 on v2

--- a/solution.py
+++ b/solution.py
@@ -36,28 +36,14 @@
     return dot3(left, right, dims) + contract(left[1], right[1], dims)
 
 
-def sources(col, hop, n_col):
-    if hop == 0 or 2 * hop == n_col:
-        return [lax.rem(col + hop, n_col)]
-    return [lax.rem(col + n_col - hop, n_col), lax.rem(col + hop, n_col)]
-
-
-def load_piece(refs):
-    if len(refs) == 1:
-        half = refs[0].shape[0] // 2
-        return jnp.concatenate([refs[0][:half], refs[0][half:]], axis=1)
-    return jnp.concatenate([refs[0][...], refs[1][...]], axis=1)
+def load_piece(ref, chunk):
+    half = ref.shape[1] // 2
+    return jnp.concatenate([ref[chunk, :half], ref[chunk, half:]], axis=1)
 
 
 def fetch(matrix_ref, window_ref, sem, chunk, long):
     start = pl.multiple_of(chunk * long, long)
     return pltpu.make_async_copy(matrix_ref.at[pl.ds(start, long)], window_ref, sem)
-
-
-def load_blocks(window_ref, rows, blocks):
-    return jnp.concatenate(
-        [window_ref[pl.ds(block, rows, stride=blocks), :] for block in range(blocks)], axis=1
-    )
 
 
 FIRST = ((0,), (0,))
@@ -89,20 +75,16 @@
     lax.fori_loop(0, chunks, step, 0)
 
 
-def collect_kernel(hop, n_col, shapes, where_ref, *refs):
-    pieces = []
-    for count in shapes:
-        pieces.append(refs[:count])
-        refs = refs[count:]
-    high_ref, low_ref, cross_ref = refs[0], refs[1], refs[-1]
-    total = None
-    for i, chunk in enumerate(sources(where_ref[0], hop, n_col)):
-        panel = split(load_piece(pieces[i]))
-        term = dot3(panel, (high_ref[chunk], low_ref[chunk]), FIRST)
-        total = term if total is None else total + term
-    for b in range(cross_ref.shape[0]):
-        term = total[:, LANES * b : LANES * (b + 1)]
-        cross_ref[b] = refs[2][b] + term if hop else term
+def collect_kernel(panel_ref, high_ref, low_ref, cross_ref):
+    cross_ref[...] = jnp.zeros_like(cross_ref)
+
+    def step(i, carry):
+        term = dot3(split(load_piece(panel_ref, i)), (high_ref[i], low_ref[i]), FIRST)
+        for b in range(cross_ref.shape[0]):
+            cross_ref[b] += term[:, LANES * b : LANES * (b + 1)]
+        return carry
+
+    lax.fori_loop(0, panel_ref.shape[0], step, 0)
 
 
 def factor_kernel(begin, end, where_ref, *refs):
@@ -193,21 +175,14 @@
         work[begin : begin + STEP, :] = jnp.where(column < begin + STEP, panel, 0.0)
 
 
-def residual_kernel(n_col, blocks, scale, shapes, where_ref, *refs):
-    pieces = []
-    for count in shapes:
-        pieces.append(refs[:count])
-        refs = refs[count:]
-    matrix_ref, mine_ref, other_ref, inverse_ref = refs[:4]
-    rows_ref, out_ref, window, result, cross, high, low, sems, out_sems = refs[4:]
-    col, core, x = where_ref[0], where_ref[1], where_ref[2]
+def residual_kernel(blocks, scale, where_ref, *refs):
+    panel_ref, matrix_ref, mine_ref, other_ref, inverse_ref = refs[:5]
+    rows_ref, out_ref, window, result, cross, sems, out_sems = refs[5:]
+    core, x = where_ref[1], where_ref[2]
     chunks, long = window.shape[0], window.shape[1]
     rows = long // blocks
     for i in range(chunks):
         fetch(matrix_ref, window.at[i], sems.at[i], i, long).start()
-    order = sum([sources(col, hop, n_col) for hop in range(n_col // 2 + 1)], [])
-    for piece, chunk in zip(pieces, order):
-        high[chunk], low[chunk] = split(load_piece(piece))
     quarters, quarter = mine_ref.shape[0], mine_ref.shape[1]
     for hop in range(quarters):
         spot = lax.rem(x + quarters - hop, quarters)
@@ -233,7 +208,8 @@
         )
 
     def step(i, carry):
-        fit = dot3((high[i], low[i]), (high_weights, low_weights), ((1,), (0,)))
+        panel = split(load_piece(panel_ref, i))
+        fit = dot3(panel, (high_weights, low_weights), ((1,), (0,)))
         fetch(matrix_ref, window.at[i], sems.at[i], i, long).wait()
         for block in range(blocks):
             result[i, pl.ds(block, rows, stride=blocks), :] = (
@@ -347,21 +323,6 @@
         name="stage",
     )(flat)
 
-    def collect(hop, pieces, *state):
-        shapes = [len(p) for p in pieces]
-        return pl.pallas_call(
-            functools.partial(collect_kernel, hop, n_col, shapes),
-            out_shape=cross_shape,
-            in_specs=[SMEM] + [VMEM] * (sum(shapes) + 2 + len(state)),
-            out_specs=VMEM,
-            compiler_params=pltpu.CompilerParams(vmem_limit_bytes=8 << 20),
-            cost_estimate=estimate(
-                6 * len(pieces) * rows * size * blocks * width,
-                4 * len(pieces) * long * width,
-            ),
-            name="collect",
-        )(where, *sum(pieces, []), *staged, *state)
-
     def factor(begin, *given):
         start = begin == 0
         return pl.pallas_call(
@@ -375,8 +336,6 @@
             name="factor",
         )(where, *given)
 
-    up = [(c, (c + 1) % n_col) for c in range(n_col)]
-    down = [(c, (c - 1) % n_col) for c in range(n_col)]
     flips = [[(c, c ^ bit) for c in range(n_col)] for bit in (4, 2, 1)]
     swap, along_x, along_y = perms
     piece = hand_out(matrix[:, 0, 0, :], spots, hits, n_col)
@@ -390,75 +349,53 @@
         cost_estimate=estimate(8 * rows * size * width, 4 * rows * size),
         name="gram",
     )(piece)
-    every = [[piece]]
-
-    left, right = lax.ppermute(piece, "col", up), lax.ppermute(piece, "col", down)
+    panel = lax.all_gather(piece, "col")
     pair = gram.reshape(2, -1, width)
     mine = pick(pair, this) + lax.ppermute(pick(pair, that), "row", swap)
-    got = send(mine, along_x)
-    cross = collect(0, [[piece]])
-    left, right, cross = lax.optimization_barrier((left, right, cross))
-    every += [[left], [right]]
-
-    left, right = lax.ppermute(left, "col", up), lax.ppermute(right, "col", down)
-    mine = total(mine, got)
-    got = send(mine, along_y)
-    cross = collect(1, every[1:3], cross)
-    left, right, cross, mine = lax.optimization_barrier((left, right, cross, mine))
-    every += [[left], [right]]
-
-    left, right = lax.ppermute(left, "col", up), lax.ppermute(right, "col", down)
-    mine = total(mine, got)
-    got = lax.ppermute(mine, "col", flips[0])
-    cross = collect(2, every[3:5], cross)
-    left, right, cross, mine = lax.optimization_barrier((left, right, cross, mine))
-    every += [[left], [right]]
-
-    last = [
-        lax.ppermute(left[:rows], "col", up),
-        lax.ppermute(right[rows:], "col", down),
-    ]
-    mine = mine + got
-    got = lax.ppermute(mine, "col", flips[1])
-    cross = collect(3, every[5:7], cross)
-    *last, cross, mine, got = lax.optimization_barrier((*last, cross, mine, got))
-    every += [last]
-
-    mine = mine + got
-    got = lax.ppermute(mine, "col", flips[2])
-    cross = collect(4, [last], cross)
+    mine = total(mine, send(mine, along_x))
+    mine = total(mine, send(mine, along_y))
+    for flip in flips:
+        mine = mine + lax.ppermute(mine, "col", flip)
+    other = lax.ppermute(mine, "row", swap)
+    work = factor(0, mine, other)
+    work = factor(SPAN, work)
+    panel, work = lax.optimization_barrier((panel, work))
+    cross = pl.pallas_call(
+        collect_kernel,
+        out_shape=cross_shape,
+        in_specs=[VMEM] * 3,
+        out_specs=VMEM,
+        compiler_params=pltpu.CompilerParams(vmem_limit_bytes=12 << 20),
+        cost_estimate=estimate(
+            6 * rows_here * size * blocks * width, 4 * rows_here * (size + blocks * width)
+        ),
+        name="collect",
+    )(panel, *staged)
     whole = cross.reshape(2, nx, -1, width)
     part = pick(whole, this) + lax.ppermute(pick(whole, that), "row", swap)
     took = [
         lax.ppermute(pick(part, steps[s + 1]), "row", p) for s, p in enumerate(along_x)
     ]
-    mine = mine + after(got, part)
-    other = lax.ppermute(mine, "row", swap)
     part = total(pick(part, steps[0]), took)
     took = send(part, along_y)
-    work = factor(SPAN, factor(0, mine, after(other, part)))
+    work = factor(2 * SPAN, after(work, part))
     part = after(total(part, took), work)
     took = send(part, along_x)
-    work = factor(3 * SPAN, factor(2 * SPAN, after(work, part)))
+    work = factor(3 * SPAN, after(work, part))
     cross_mine = after(jnp.stack([part, *took]), work)
     cross_other = lax.ppermute(cross_mine, "row", swap)
-    shapes = [len(p) for p in every]
     scaled, residual = pl.pallas_call(
-        functools.partial(
-            residual_kernel, n_col, blocks, 1.0 / math.sqrt(rows_here * n_row), shapes
-        ),
+        functools.partial(residual_kernel, blocks, 1.0 / math.sqrt(rows_here * n_row)),
         out_shape=(
             shape((size * blocks, width), f32),
             shape((rows_here * blocks, width), f32),
         ),
-        in_specs=[SMEM] + [VMEM] * sum(shapes) + [HBM, VMEM, VMEM, VMEM],
+        in_specs=[SMEM, VMEM, HBM, VMEM, VMEM, VMEM],
         out_specs=(VMEM, HBM),
         scratch_shapes=[
             pltpu.VMEM((n_col, long, width), f32),
             pltpu.VMEM((n_col, long, width), f32),
             pltpu.VMEM((size * blocks, width), f32),
-            pltpu.VMEM((n_col, rows, size), jnp.bfloat16),
-            pltpu.VMEM((n_col, rows, size), jnp.bfloat16),
             pltpu.SemaphoreType.DMA((n_col,)),
             pltpu.SemaphoreType.DMA((n_col,)),
         ],
@@ -467,7 +404,7 @@
             6 * rows_here * size * blocks * width, 4 * rows_here * (size + 2 * blocks * width)
         ),
         name="residual",
-    )(where, *sum(every, []), flat, cross_mine, cross_other, work)
+    )(where, panel, flat, cross_mine, cross_other, work)
     return (
         scaled.reshape(size, blocks, 1, width),
         residual.reshape(rows_here, blocks, 1, width),

time: 120 us -> 148 us (1.23)
  waiting for transfers between devices: 23.7 us -> 51 us
  starting transfers between devices: 61.1 us -> 44.7 us
  between operations: 1.28 us -> 14.4 us
  local copies, waits for them, and re-layouts: 4.25 us -> 9.98 us
  Pallas kernels: 28.8 us -> 26.6 us
    ppermute x12, waiting for transfers between devices: 0.03 us -> 13.8 us  [send(): return [lax.ppermute(value, 'row', perm) for perm in perms]]
    ppermute x11 -> x3, starting transfers between devices: 12.8 us -> 0.28 us  [per_device(): mine = mine + lax.ppermute(mine, 'col', flip)]
    ppermute x11 -> x3, waiting for transfers between devices: 11.1 us -> 22.6 us  [per_device(): mine = mine + lax.ppermute(mine, 'col', flip)]
    ppermute x1, starting transfers between devices: 6.75 us -> 0.44 us  [per_device(): part = pick(whole, this) + lax.ppermute(pick(whole, that), 'row', swap)]
    unnamed x0 -> x10, local copies, waits for them, and re-layouts: none -> 5.76 us
    ppermute x1, starting transfers between devices: 1.3 us -> 5.03 us  [per_device(): other = lax.ppermute(mine, 'row', swap)]
    ppermute x3, starting transfers between devices: 4.28 us -> 1.99 us  [per_device(): lax.ppermute(pick(part, steps[s + 1]), 'row', p)]
    pallas_call x6 -> x2, Pallas kernels: 14.9 us -> 12.6 us  [the longest x1 8.41 us: per_device(): pl.pallas_call(functools.partial(residual_kernel, blocks, 1.0 / math.sqrt...]
  transfers between devices with their start and end apart: 37 -> 30, of which waited for: 12 -> 18; matrix products, arithmetic and copies ran while one was open for 3% -> 2% of each run, Pallas kernels for 16% -> 9%
where the time goes in v3:
time: 148 us
  waiting for transfers between devices  51 us (34%)
  starting transfers between devices  44.7 us (30%)
  Pallas kernels  26.6 us (18%)
  between operations  14.4 us (10%)
  local copies, waits for them, and re-layouts  9.98 us (7%)
    ppermute x3, waiting for transfers between devices, per_device(): mine = mine + lax.ppermute(mine, 'col', flip)  22.6 us
    ppermute x7, starting transfers between devices, hand_out(): got = lax.ppermute(pick(pieces, spots[s]), 'col', pairs)  16.8 us
    ppermute x12, starting transfers between devices, send(): return [lax.ppermute(value, 'row', perm) for perm in perms]  14.5 us
    ppermute x12, waiting for transfers between devices, send(): return [lax.ppermute(value, 'row', perm) for perm in perms]  13.8 us
    pallas_call x4, Pallas kernels, factor(): pl.pallas_call(functools.partial(factor_kernel, begin, begin + SPAN), out...  10.9 us
    pallas_call x1, Pallas kernels, per_device(): pl.pallas_call(functools.partial(residual_kernel, blocks, 1.0 / math.sqrt...  8.41 us
    unnamed x10, local copies, waits for them, and re-layouts  5.76 us
    ppermute x7, waiting for transfers between devices, hand_out(): got = lax.ppermute(pick(pieces, spots[s]), 'col', pairs)  5.7 us
  transfers between devices with their start and end apart: 30, of which 18 were waited for; matrix products, arithmetic and copies ran while one was open for 2% of the time, Pallas kernels for 9%

profile of v3, /device:TPU:1, one launch (start us, length us, event | category | flops | bytes accessed | tf_op | source)
XLA Modules:
  0.0 147.7 jit_solution(9294257391713750027)
XLA Ops:
  8.7 4.4 %collective-permute-start.6 = (f32[256,128]{1,0:T(8,128)S(1)}, f32[256,128]{1,0:T(8,128)S(1)}, u32[]{:S(2)}, u32[]{:S(2)}) collective-permute-start(f32[256,128]{1,0:T(8,128)S(1)} %get-tuple-element.80), channel_id=1, source_target_pairs={{0,1},{1,2},{8,9},{9,10},{16,17},{17,18},{24,25},{25,26},{32,33},{... | collective-permute-start | bytes 393224 | tf_op jit(solution)/shard_map/ppermute | solution.py:271
  13.1 2.6 %collective-permute-start.5 = (f32[256,128]{1,0:T(8,128)S(1)}, f32[256,128]{1,0:T(8,128)S(1)}, u32[]{:S(2)}, u32[]{:S(2)}) collective-permute-start(f32[256,128]{1,0:T(8,128)S(1)} %get-tuple-element.81), channel_id=1, source_target_pairs={{0,2},{1,3},{8,10},{9,11},{16,18},{17,19},{24,26},{25,27},{32,34},... | collective-permute-start | bytes 393224 | tf_op jit(solution)/shard_map/ppermute | solution.py:271
  15.7 2.0 %collective-permute-start.4 = (f32[256,128]{1,0:T(8,128)S(1)}, f32[256,128]{1,0:T(8,128)S(1)}, u32[]{:S(2)}, u32[]{:S(2)}) collective-permute-start(f32[256,128]{1,0:T(8,128)S(1)} %get-tuple-element.82), channel_id=1, source_target_pairs={{0,3},{1,4},{8,11},{9,12},{16,19},{17,20},{24,27},{25,28},{32,35},... | collective-permute-start | bytes 393224 | tf_op jit(solution)/shard_map/ppermute | solution.py:271
  17.8 3.2 %collective-permute-start.3 = (f32[256,128]{1,0:T(8,128)S(1)}, f32[256,128]{1,0:T(8,128)S(1)}, u32[]{:S(2)}, u32[]{:S(2)}) collective-permute-start(f32[256,128]{1,0:T(8,128)S(1)} %get-tuple-element.83), channel_id=1, source_target_pairs={{0,4},{1,5},{8,12},{9,13},{16,20},{17,21},{24,28},{25,29},{32,36},... | collective-permute-start | bytes 393224 | tf_op jit(solution)/shard_map/ppermute | solution.py:271
  25.6 2.8 %copy.7 = f32[2048,5,1,128]{3,0,2,1:T(8,128)S(1)} copy(f32[2048,5,1,128]{3,2,1,0:T(1,128)} %param.1) | data formatting | bytes 10485760 | tf_op jit(solution)/shard_map/optimization_barrier | solution.py:299
  28.4 2.7 %stage.1 = (bf16[8,256,640]{2,1,0:T(8,128)(2,1)S(1)}, bf16[8,256,640]{2,1,0:T(8,128)(2,1)S(1)}) custom-call(f32[10240,128]{1,0:T(8,128)} %bitcast.84), custom_call_target="tpu_custom_call" | custom-call | flops 10485760 | bytes 10485760 | tf_op jit(solution)/shard_map/stage/pallas_call | solution.py:312
  32.6 2.9 %collective-permute-done.1 = f32[256,128]{1,0:T(8,128)S(1)} collective-permute-done((f32[256,128]{1,0:T(8,128)S(1)}, f32[256,128]{1,0:T(8,128)S(1)}, u32[]{:S(2)}, u32[]{:S(2)}) %collective-permute-start.1) | collective-permute-done | bytes 131104 | tf_op jit(solution)/shard_map/ppermute | solution.py:271
  35.4 2.8 %collective-permute-done = f32[256,128]{1,0:T(8,128)S(1)} collective-permute-done((f32[256,128]{1,0:T(8,128)S(1)}, f32[256,128]{1,0:T(8,128)S(1)}, u32[]{:S(2)}, u32[]{:S(2)}) %collective-permute-start) | collective-permute-done | bytes 131104 | tf_op jit(solution)/shard_map/ppermute | solution.py:271
  42.0 2.6 %collective-permute-start.10 = (f32[192,128]{1,0:T(8,128)S(1)}, f32[192,128]{1,0:T(8,128)S(1)}, u32[]{:S(2)}, u32[]{:S(2)}) collective-permute-start(f32[192,128]{1,0:T(8,128)S(1)} %bitcast_add_fusion.1), channel_id=1, source_target_pairs={{0,192},{8,200},{16,208},{24,216},{32,224},{40,232},{48,240},{56,2... | collective-permute-start | bytes 294920 | tf_op jit(solution)/shard_map/ppermute | solution.py:259
  46.4 5.6 %collective-permute-done.9 = f32[192,128]{1,0:T(8,128)S(1)} collective-permute-done((f32[192,128]{1,0:T(8,128)S(1)}, f32[192,128]{1,0:T(8,128)S(1)}, u32[]{:S(2)}, u32[]{:S(2)}) %collective-permute-start.9) | collective-permute-done | bytes 98336 | tf_op jit(solution)/shard_map/ppermute | solution.py:259
  52.0 2.8 %collective-permute-start.13 = (f32[192,128]{1,0:T(8,128)S(1)}, f32[192,128]{1,0:T(8,128)S(1)}, u32[]{:S(2)}, u32[]{:S(2)}) collective-permute-start(f32[192,128]{1,0:T(8,128)S(1)} %add_add_fusion.1), channel_id=1, source_target_pairs={{0,48},{8,56},{16,0},{24,8},{32,16},{40,24},{48,32},{56,40},{64,11... | collective-permute-start | bytes 294920 | tf_op jit(solution)/shard_map/ppermute | solution.py:259
  56.5 4.5 %collective-permute-done.12 = f32[192,128]{1,0:T(8,128)S(1)} collective-permute-done((f32[192,128]{1,0:T(8,128)S(1)}, f32[192,128]{1,0:T(8,128)S(1)}, u32[]{:S(2)}, u32[]{:S(2)}) %collective-permute-start.12) | collective-permute-done | bytes 98336 | tf_op jit(solution)/shard_map/ppermute | solution.py:259
  61.1 10.7 %collective-permute-done.14 = f32[192,128]{1,0:T(8,128)S(1)} collective-permute-done((f32[192,128]{1,0:T(8,128)S(1)}, f32[192,128]{1,0:T(8,128)S(1)}, u32[]{:S(2)}, u32[]{:S(2)}) %collective-permute-start.14) | collective-permute-done | bytes 98336 | tf_op jit(solution)/shard_map/ppermute | solution.py:358
  71.9 7.6 %collective-permute-done.15 = f32[192,128]{1,0:T(8,128)S(1)} collective-permute-done((f32[192,128]{1,0:T(8,128)S(1)}, f32[192,128]{1,0:T(8,128)S(1)}, u32[]{:S(2)}, u32[]{:S(2)}) %collective-permute-start.15) | collective-permute-done | bytes 98336 | tf_op jit(solution)/shard_map/ppermute | solution.py:358
  79.6 4.4 %collective-permute-done.16 = f32[192,128]{1,0:T(8,128)S(1)} collective-permute-done((f32[192,128]{1,0:T(8,128)S(1)}, f32[192,128]{1,0:T(8,128)S(1)}, u32[]{:S(2)}, u32[]{:S(2)}) %collective-permute-start.16) | collective-permute-done | bytes 98336 | tf_op jit(solution)/shard_map/ppermute | solution.py:358
  84.0 5.0 %collective-permute-start.17 = (f32[192,128]{1,0:T(8,128)S(1)}, f32[192,128]{1,0:T(8,128)S(1)}, u32[]{:S(2)}, u32[]{:S(2)}) collective-permute-start(f32[192,128]{1,0:T(8,128)S(1)} %add.101.refs_0_), channel_id=1, source_target_pairs={{0,8},{8,0},{16,24},{24,16},{32,40},{40,32},{48,56},{56,48},{64,72... | collective-permute-start | bytes 294920 | tf_op jit(solution)/shard_map/ppermute | solution.py:359
  90.0 2.9 %factor.4.refs_0_ = f32[256,256]{1,0:T(8,128)S(1)} custom-call(s32[3]{0:T(128)S(1)} %pad_add_fusion.where_ref, f32[192,128]{1,0:T(8,128)S(1)} %add.101.refs_0_, f32[192,128]{1,0:T(8,128)S(1)} %collective-permute-done.17.refs_1_), custom_call_target="tpu_custom_call" | custom-call | flops 4294967296 | bytes 524288 | tf_op jit(solution)/shard_map/factor/pallas_call | solution.py:328
  92.9 2.8 %factor.5.refs_0_ = f32[256,256]{1,0:T(8,128)S(1)} custom-call(s32[3]{0:T(128)S(1)} %pad_add_fusion.where_ref, f32[256,256]{1,0:T(8,128)S(1)} %factor.4.refs_0_), custom_call_target="tpu_custom_call" | custom-call | flops 4294967296 | bytes 524288 | tf_op jit(solution)/shard_map/factor/pallas_call | solution.py:328
  99.0 4.2 %collect.1 = f32[5,256,128]{2,1,0:T(8,128)S(1)} custom-call(f32[8,512,128]{2,1,0:T(8,128)S(1)} %bitcast.78, bf16[8,256,640]{2,1,0:T(8,128)(2,1)S(1)} %get-tuple-element.61.high_ref, bf16[8,256,640]{2,1,0:T(8,128)(2,1)S(1)} %copy-done.3), custom_call_target="tpu_custom_call" | custom-call | flops 2013265920 | bytes 7340032 | tf_op jit(solution)/shard_map/collect/pallas_call | solution.py:363
  111.5 2.1 %collective-permute-start.24 = (f32[160,128]{1,0:T(8,128)S(1)}, f32[160,128]{1,0:T(8,128)S(1)}, u32[]{:S(2)}, u32[]{:S(2)}) collective-permute-start(f32[160,128]{1,0:T(8,128)S(1)} %fusion.14), channel_id=1, source_target_pairs={{0,48},{8,56},{16,0},{24,8},{32,16},{40,24},{48,32},{56,40},{64,11... | collective-permute-start | bytes 245768 | tf_op jit(solution)/shard_map/ppermute | solution.py:259
  114.8 2.8 %factor.6.refs_0_ = f32[256,256]{1,0:T(8,128)S(1)} custom-call(s32[3]{0:T(128)S(1)} %pad_add_fusion.where_ref, f32[256,256]{1,0:T(8,128)S(1)} %factor.5.refs_0_), custom_call_target="tpu_custom_call" | custom-call | flops 4294967296 | bytes 524288 | tf_op jit(solution)/shard_map/factor/pallas_call | solution.py:328
  121.5 2.5 %factor.7.refs_4_ = f32[256,256]{1,0:T(8,128)S(1)} custom-call(s32[3]{0:T(128)S(1)} %pad_add_fusion.where_ref, f32[256,256]{1,0:T(8,128)S(1)} %factor.6.refs_0_), custom_call_target="tpu_custom_call" | custom-call | flops 4294967296 | bytes 524288 | tf_op jit(solution)/shard_map/factor/pallas_call | solution.py:328
  126.2 5.0 %collective-permute-start.28 = (f32[4,160,128]{2,1,0:T(8,128)S(1)}, f32[4,160,128]{2,1,0:T(8,128)S(1)}, u32[]{:S(2)}, u32[]{:S(2)}) collective-permute-start(f32[4,160,128]{2,1,0:T(8,128)S(1)} %pad_maximum_fusion.refs_2_), channel_id=1, source_target_pairs={{0,8},{8,0},{16,24},{24,16},{32,40},{40,32},{48,56},{56,48},{64,72... | collective-permute-start | bytes 983048 | tf_op jit(solution)/shard_map/ppermute | solution.py:386
  132.5 8.4 %residual.1 = (f32[1280,128]{1,0:T(8,128)}, f32[10240,128]{1,0:T(8,128)}) custom-call(s32[3]{0:T(128)S(1)} %pad_add_fusion.where_ref, f32[8,512,128]{2,1,0:T(8,128)S(1)} %bitcast.79, f32[10240,128]{1,0:T(8,128)} %bitcast.85, f32[4,160,128]{2,1,0:T(8,128)S(1)} %pad_maximum_fusion.refs_2_, f32[4,160,128]{2,1,0:T(8,128)S(1)} %collective-permute-done.28.refs_3_, ...), custom_call_target="tpu_custom_call" | custom-call | flops 2013265920 | bytes 12582912 | tf_op jit(solution)/shard_map/residual/pallas_call | solution.py:387
  (74 shorter events, 36.1 us)
Async XLA Ops:
  7.2 88.5 %all-gather.3.cloned.1.call-start = ((), (), s32[]{:S(2)}) async-start(), calls=%async_computation | async-start | bytes 2359296 | tf_op jit(solution)/shard_map/all_gather | solution.py:352
  8.7 13.6 %collective-permute-start.6 = (f32[256,128]{1,0:T(8,128)S(1)}, f32[256,128]{1,0:T(8,128)S(1)}, u32[]{:S(2)}, u32[]{:S(2)}) collective-permute-start(f32[256,128]{1,0:T(8,128)S(1)} %get-tuple-element.80), channel_id=1, source_target_pairs={{0,1},{1,2},{8,9},{9,10},{16,17},{17,18},{24,25},{25,26},{32,33},{... | collective-permute-start | bytes 393224 | tf_op jit(solution)/shard_map/ppermute | solution.py:271
  13.1 10.5 %collective-permute-start.5 = (f32[256,128]{1,0:T(8,128)S(1)}, f32[256,128]{1,0:T(8,128)S(1)}, u32[]{:S(2)}, u32[]{:S(2)}) collective-permute-start(f32[256,128]{1,0:T(8,128)S(1)} %get-tuple-element.81), channel_id=1, source_target_pairs={{0,2},{1,3},{8,10},{9,11},{16,18},{17,19},{24,26},{25,27},{32,34},... | collective-permute-start | bytes 393224 | tf_op jit(solution)/shard_map/ppermute | solution.py:271
  15.7 16.8 %collective-permute-start.4 = (f32[256,128]{1,0:T(8,128)S(1)}, f32[256,128]{1,0:T(8,128)S(1)}, u32[]{:S(2)}, u32[]{:S(2)}) collective-permute-start(f32[256,128]{1,0:T(8,128)S(1)} %get-tuple-element.82), channel_id=1, source_target_pairs={{0,3},{1,4},{8,11},{9,12},{16,19},{17,20},{24,27},{25,28},{32,35},... | collective-permute-start | bytes 393224 | tf_op jit(solution)/shard_map/ppermute | solution.py:271
  17.8 14.8 %collective-permute-start.3 = (f32[256,128]{1,0:T(8,128)S(1)}, f32[256,128]{1,0:T(8,128)S(1)}, u32[]{:S(2)}, u32[]{:S(2)}) collective-permute-start(f32[256,128]{1,0:T(8,128)S(1)} %get-tuple-element.83), channel_id=1, source_target_pairs={{0,4},{1,5},{8,12},{9,13},{16,20},{17,21},{24,28},{25,29},{32,36},... | collective-permute-start | bytes 393224 | tf_op jit(solution)/shard_map/ppermute | solution.py:271
  21.0 11.6 %collective-permute-start.2 = (f32[256,128]{1,0:T(8,128)S(1)}, f32[256,128]{1,0:T(8,128)S(1)}, u32[]{:S(2)}, u32[]{:S(2)}) collective-permute-start(f32[256,128]{1,0:T(8,128)S(1)} %get-tuple-element.84), channel_id=1, source_target_pairs={{0,5},{1,6},{8,13},{9,14},{16,21},{17,22},{24,29},{25,30},{32,37},... | collective-permute-start | bytes 393224 | tf_op jit(solution)/shard_map/ppermute | solution.py:271
  22.3 13.1 %collective-permute-start.1 = (f32[256,128]{1,0:T(8,128)S(1)}, f32[256,128]{1,0:T(8,128)S(1)}, u32[]{:S(2)}, u32[]{:S(2)}) collective-permute-start(f32[256,128]{1,0:T(8,128)S(1)} %get-tuple-element.85), channel_id=1, source_target_pairs={{0,6},{1,7},{8,14},{9,15},{16,22},{17,23},{24,30},{25,31},{32,38},... | collective-permute-start | bytes 393224 | tf_op jit(solution)/shard_map/ppermute | solution.py:271
  23.6 14.6 %collective-permute-start = (f32[256,128]{1,0:T(8,128)S(1)}, f32[256,128]{1,0:T(8,128)S(1)}, u32[]{:S(2)}, u32[]{:S(2)}) collective-permute-start(f32[256,128]{1,0:T(8,128)S(1)} %get-tuple-element.86), channel_id=1, source_target_pairs={{0,7},{1,0},{8,15},{9,8},{16,23},{17,16},{24,31},{25,24},{32,39},{... | collective-permute-start | bytes 393224 | tf_op jit(solution)/shard_map/ppermute | solution.py:271
  44.6 7.4 %collective-permute-start.9 = (f32[192,128]{1,0:T(8,128)S(1)}, f32[192,128]{1,0:T(8,128)S(1)}, u32[]{:S(2)}, u32[]{:S(2)}) collective-permute-start(f32[192,128]{1,0:T(8,128)S(1)} %bitcast_add_fusion.1), channel_id=1, source_target_pairs={{0,64},{8,72},{16,80},{24,88},{32,96},{40,104},{48,112},{56,120},{... | collective-permute-start | bytes 294920 | tf_op jit(solution)/shard_map/ppermute | solution.py:259
  44.6 7.4 %collective-permute-start.8 = (f32[192,128]{1,0:T(8,128)S(1)}, f32[192,128]{1,0:T(8,128)S(1)}, u32[]{:S(2)}, u32[]{:S(2)}) collective-permute-start(f32[192,128]{1,0:T(8,128)S(1)} %bitcast_add_fusion.1), channel_id=1, source_target_pairs={{0,128},{8,136},{16,144},{24,152},{32,160},{40,168},{48,176},{56,1... | collective-permute-start | bytes 294920 | tf_op jit(solution)/shard_map/ppermute | solution.py:259
  54.8 6.2 %collective-permute-start.12 = (f32[192,128]{1,0:T(8,128)S(1)}, f32[192,128]{1,0:T(8,128)S(1)}, u32[]{:S(2)}, u32[]{:S(2)}) collective-permute-start(f32[192,128]{1,0:T(8,128)S(1)} %add_add_fusion.1), channel_id=1, source_target_pairs={{0,16},{8,24},{16,32},{24,40},{32,48},{40,56},{48,0},{56,8},{64,80... | collective-permute-start | bytes 294920 | tf_op jit(solution)/shard_map/ppermute | solution.py:259
  54.8 6.2 %collective-permute-start.11 = (f32[192,128]{1,0:T(8,128)S(1)}, f32[192,128]{1,0:T(8,128)S(1)}, u32[]{:S(2)}, u32[]{:S(2)}) collective-permute-start(f32[192,128]{1,0:T(8,128)S(1)} %add_add_fusion.1), channel_id=1, source_target_pairs={{0,32},{8,40},{16,48},{24,56},{32,0},{40,8},{48,16},{56,24},{64,96... | collective-permute-start | bytes 294920 | tf_op jit(solution)/shard_map/ppermute | solution.py:259
  61.0 10.8 %collective-permute-start.14 = (f32[192,128]{1,0:T(8,128)S(1)}, f32[192,128]{1,0:T(8,128)S(1)}, u32[]{:S(2)}, u32[]{:S(2)}) collective-permute-start(f32[192,128]{1,0:T(8,128)S(1)} %add_add_fusion), channel_id=1, source_target_pairs={{0,4},{1,5},{2,6},{3,7},{4,0},{5,1},{6,2},{7,3},{8,12},{9,13},{10,... | collective-permute-start | bytes 294920 | tf_op jit(solution)/shard_map/ppermute | solution.py:358
  71.8 7.7 %collective-permute-start.15 = (f32[192,128]{1,0:T(8,128)S(1)}, f32[192,128]{1,0:T(8,128)S(1)}, u32[]{:S(2)}, u32[]{:S(2)}) collective-permute-start(f32[192,128]{1,0:T(8,128)S(1)} %add.99), channel_id=1, source_target_pairs={{0,2},{1,3},{2,0},{3,1},{4,6},{5,7},{6,4},{7,5},{8,10},{9,11},{10,... | collective-permute-start | bytes 294920 | tf_op jit(solution)/shard_map/ppermute | solution.py:358
  84.0 6.0 %collective-permute-start.17 = (f32[192,128]{1,0:T(8,128)S(1)}, f32[192,128]{1,0:T(8,128)S(1)}, u32[]{:S(2)}, u32[]{:S(2)}) collective-permute-start(f32[192,128]{1,0:T(8,128)S(1)} %add.101.refs_0_), channel_id=1, source_target_pairs={{0,8},{8,0},{16,24},{24,16},{32,40},{40,32},{48,56},{56,48},{64,72... | collective-permute-start | bytes 294920 | tf_op jit(solution)/shard_map/ppermute | solution.py:359
  105.8 4.5 %collective-permute-start.20 = (f32[160,128]{1,0:T(8,128)S(1)}, f32[160,128]{1,0:T(8,128)S(1)}, u32[]{:S(2)}, u32[]{:S(2)}) collective-permute-start(f32[160,128]{1,0:T(8,128)S(1)} %get-tuple-element.88), channel_id=1, source_target_pairs={{0,64},{8,72},{16,80},{24,88},{32,96},{40,104},{48,112},{56,120},{... | collective-permute-start | bytes 245768 | tf_op jit(solution)/shard_map/ppermute | solution.py:377
  106.6 4.9 %collective-permute-start.19 = (f32[160,128]{1,0:T(8,128)S(1)}, f32[160,128]{1,0:T(8,128)S(1)}, u32[]{:S(2)}, u32[]{:S(2)}) collective-permute-start(f32[160,128]{1,0:T(8,128)S(1)} %get-tuple-element.89), channel_id=1, source_target_pairs={{0,128},{8,136},{16,144},{24,152},{32,160},{40,168},{48,176},{56,1... | collective-permute-start | bytes 245768 | tf_op jit(solution)/shard_map/ppermute | solution.py:377
  111.5 6.1 %collective-permute-start.24 = (f32[160,128]{1,0:T(8,128)S(1)}, f32[160,128]{1,0:T(8,128)S(1)}, u32[]{:S(2)}, u32[]{:S(2)}) collective-permute-start(f32[160,128]{1,0:T(8,128)S(1)} %fusion.14), channel_id=1, source_target_pairs={{0,48},{8,56},{16,0},{24,8},{32,16},{40,24},{48,32},{56,40},{64,11... | collective-permute-start | bytes 245768 | tf_op jit(solution)/shard_map/ppermute | solution.py:259
  113.6 5.4 %collective-permute-start.23 = (f32[160,128]{1,0:T(8,128)S(1)}, f32[160,128]{1,0:T(8,128)S(1)}, u32[]{:S(2)}, u32[]{:S(2)}) collective-permute-start(f32[160,128]{1,0:T(8,128)S(1)} %fusion.14), channel_id=1, source_target_pairs={{0,16},{8,24},{16,32},{24,40},{32,48},{40,56},{48,0},{56,8},{64,80... | collective-permute-start | bytes 245768 | tf_op jit(solution)/shard_map/ppermute | solution.py:259
  113.6 5.4 %collective-permute-start.22 = (f32[160,128]{1,0:T(8,128)S(1)}, f32[160,128]{1,0:T(8,128)S(1)}, u32[]{:S(2)}, u32[]{:S(2)}) collective-permute-start(f32[160,128]{1,0:T(8,128)S(1)} %fusion.14), channel_id=1, source_target_pairs={{0,32},{8,40},{16,48},{24,56},{32,0},{40,8},{48,16},{56,24},{64,96... | collective-permute-start | bytes 245768 | tf_op jit(solution)/shard_map/ppermute | solution.py:259
  119.0 4.9 %collective-permute-start.27 = (f32[160,128]{1,0:T(8,128)S(1)}, f32[160,128]{1,0:T(8,128)S(1)}, u32[]{:S(2)}, u32[]{:S(2)}) collective-permute-start(f32[160,128]{1,0:T(8,128)S(1)} %add_add_fusion.2), channel_id=1, source_target_pairs={{0,192},{8,200},{16,208},{24,216},{32,224},{40,232},{48,240},{56,2... | collective-permute-start | bytes 245768 | tf_op jit(solution)/shard_map/ppermute | solution.py:259
  120.8 4.9 %collective-permute-start.26 = (f32[160,128]{1,0:T(8,128)S(1)}, f32[160,128]{1,0:T(8,128)S(1)}, u32[]{:S(2)}, u32[]{:S(2)}) collective-permute-start(f32[160,128]{1,0:T(8,128)S(1)} %add_add_fusion.2), channel_id=1, source_target_pairs={{0,128},{8,136},{16,144},{24,152},{32,160},{40,168},{48,176},{56,1... | collective-permute-start | bytes 245768 | tf_op jit(solution)/shard_map/ppermute | solution.py:259
  120.8 5.4 %collective-permute-start.25 = (f32[160,128]{1,0:T(8,128)S(1)}, f32[160,128]{1,0:T(8,128)S(1)}, u32[]{:S(2)}, u32[]{:S(2)}) collective-permute-start(f32[160,128]{1,0:T(8,128)S(1)} %add_add_fusion.2), channel_id=1, source_target_pairs={{0,64},{8,72},{16,80},{24,88},{32,96},{40,104},{48,112},{56,120},{... | collective-permute-start | bytes 245768 | tf_op jit(solution)/shard_map/ppermute | solution.py:259
  126.2 6.3 %collective-permute-start.28 = (f32[4,160,128]{2,1,0:T(8,128)S(1)}, f32[4,160,128]{2,1,0:T(8,128)S(1)}, u32[]{:S(2)}, u32[]{:S(2)}) collective-permute-start(f32[4,160,128]{2,1,0:T(8,128)S(1)} %pad_maximum_fusion.refs_2_), channel_id=1, source_target_pairs={{0,8},{8,0},{16,24},{24,16},{32,40},{40,32},{48,56},{56,48},{64,72... | collective-permute-start | bytes 983048 | tf_op jit(solution)/shard_map/ppermute | solution.py:386
  (11 other events, 39.5 us)
Sparse Core Ops, SparseCore 0:
  39.2 40.6 all-gather.2
